TPU v7x, 512 devices: a whole 4x8x8 slice. The times are simulated.
512 devices in a mesh: ens: 32 (over z, y_lo, core), pen: 16 (over x, y_hi).
Axes of the slice: x: 4, y: 8 (y_hi: 4, y_lo: 2; y = y_hi * 2 + y_lo), z: 8, core: 2. Of those that a mesh axis runs over, the one named last changes fastest.
Arguments:
- state: float32 [2, 32, 4, 256, 512], P(None, 'ens', None, 'pen'), may hold values from -8 to 8, as said below
- accum: float32 [2, 32, 4, 256, 512], P(None, 'ens', None, 'pen'), may hold values from -8 to 8, as said below
- base_flow: float32 [6, 4, 256, 256], P(None, None, 'pen', 'ens'), may hold values from -6 to 6
Outputs:
- state_next: float32 [2, 32, 4, 256, 512], P(None, 'ens', None, 'pen')
- accum_next: float32 [2, 32, 4, 256, 512], P(None, 'ens', None, 'pen')
Inputs may be any that keep to these rules, and one draw needn't show every extreme that they name: `state`: each field of each perturbation and level is the spectrum of a real field: the entry at ((256 - ky) mod 256, (256 - kx) mod 256) is the complex conjugate of the entry at (ky, kx). `accum`: each field of each perturbation and level is the spectrum of a real field: the entry at ((256 - ky) mod 256, (256 - kx) mod 256) is the complex conjugate of the entry at (ky, kx).
All inputs are finite; a program needn't handle non-finite values.
Results may differ from a plain program's by a relative error of at most 0.0003.
Values sent between devices are 32-bit elements; how exact they have to be, the bound alone decides.
A program may use at most 64 MiB of HBM per device.

v0:
```python
import math

import jax
import jax.numpy as jnp
from jax import lax
from jax.sharding import PartitionSpec as P

viscosity = 0.05
diffusivity = 0.05
vertical_mixing = 0.5
buoyancy_gain = 0.5
stratification = 0.5
memory_factor = -5.0 / 9.0
weight_factor = 15.0 / 16.0
time_step = 0.4


def wave_numbers(amount, offset, length):
    position = offset + jnp.arange(amount, dtype=jnp.int32)
    half_length = length // 2
    signed = jnp.where(position <= half_length, position, position - length)
    derivative = jnp.where(position == half_length, 0, signed)
    return (2.0 * math.pi / length * derivative.astype(jnp.float32), signed)


def times_i(real_part, imag_part, factor):
    return (-factor * imag_part, factor * real_part)


def vertical(quantity, level_axis):
    depth = quantity.shape[level_axis]
    lower = lax.slice_in_dim(quantity, 0, 1, axis=level_axis)
    upper = lax.slice_in_dim(quantity, depth - 1, depth, axis=level_axis)
    padded = jnp.concatenate([lower, quantity, upper], axis=level_axis)
    above = lax.slice_in_dim(padded, 2, depth + 2, axis=level_axis)
    below = lax.slice_in_dim(padded, 0, depth, axis=level_axis)
    return above + below - 2.0 * quantity


def tendency(vort, buoy, advect, across, kappa_x, square, level_axis):
    tend_vort_re = (
        -advect[0]
        + buoyancy_gain * (-kappa_x * buoy[1])
        - viscosity * square * vort[0]
        + vertical_mixing * vertical(vort[0], level_axis)
    )
    tend_vort_im = (
        -advect[1]
        + buoyancy_gain * (kappa_x * buoy[0])
        - viscosity * square * vort[1]
        + vertical_mixing * vertical(vort[1], level_axis)
    )
    tend_buoy_re = (
        -advect[2]
        - stratification * across[0]
        - diffusivity * square * buoy[0]
        + vertical_mixing * vertical(buoy[0], level_axis)
    )
    tend_buoy_im = (
        -advect[3]
        - stratification * across[1]
        - diffusivity * square * buoy[1]
        + vertical_mixing * vertical(buoy[1], level_axis)
    )
    return jnp.stack(
        [
            jnp.concatenate([tend_vort_re, tend_vort_im], axis=-1),
            jnp.concatenate([tend_buoy_re, tend_buoy_im], axis=-1),
        ]
    )


def dft_tables(length):
    position = jnp.arange(length, dtype=jnp.int32)
    product = position[:, None] * position[None, :] % length
    angle = 2.0 * math.pi / length * product.astype(jnp.float32)
    scale = 1.0 / math.sqrt(length)
    return (scale * jnp.cos(angle), scale * jnp.sin(angle))


def to_physical(spectral, x_table, y_table):
    mixed_space = jnp.einsum(
        "fplkj,jcx->fplcxk", spectral, x_table, precision=lax.Precision.HIGHEST
    )
    return jnp.einsum(
        "fplcxk,ckm->fplxm",
        lax.all_to_all(mixed_space, "pen", split_axis=4, concat_axis=5, tiled=True),
        y_table,
        precision=lax.Precision.HIGHEST,
    )


def on_device(state, accum, base_flow):
    grid_size = state.shape[-1] // 2
    row_count = state.shape[3]
    base_all = lax.all_gather(base_flow, "ens", axis=3, tiled=True)
    kappa_rows, signed_y = wave_numbers(row_count, lax.axis_index("pen") * row_count, grid_size)
    kappa_cols, signed_x = wave_numbers(grid_size, 0, grid_size)
    kappa_y = kappa_rows[:, None]
    kappa_x = kappa_cols[None, :]
    wave_square = signed_y[:, None] ** 2 + signed_x[None, :] ** 2
    factor = (2.0 * math.pi / grid_size) ** 2
    square = factor * wave_square.astype(jnp.float32)
    inverse = jnp.where(
        wave_square > 0, 1.0 / (factor * jnp.maximum(wave_square, 1).astype(jnp.float32)), 0.0
    )
    vort = (state[0][..., :grid_size], state[0][..., grid_size:])
    buoy = (state[1][..., :grid_size], state[1][..., grid_size:])
    potential_re = -vort[0] * inverse
    potential_im = -vort[1] * inverse
    flow_x = times_i(potential_re, potential_im, -kappa_y)
    flow_y = times_i(potential_re, potential_im, kappa_x)
    vort_x = times_i(vort[0], vort[1], kappa_x)
    vort_y = times_i(vort[0], vort[1], kappa_y)
    buoy_x = times_i(buoy[0], buoy[1], kappa_x)
    buoy_y = times_i(buoy[0], buoy[1], kappa_y)
    cosine_table, sine_table = dft_tables(grid_size)
    x_table = jnp.concatenate(
        [
            jnp.stack([cosine_table, sine_table], axis=1),
            jnp.stack([-sine_table, cosine_table], axis=1),
        ],
        axis=0,
    )
    y_table = jnp.stack([cosine_table, -sine_table])
    components = [flow_x, flow_y, vort_x, vort_y, buoy_x, buoy_y]
    spectral = jnp.stack([jnp.concatenate(component, axis=-1) for component in components])
    physical = to_physical(spectral, x_table, y_table)
    flow_x_p, flow_y_p = (physical[0], physical[1])
    vort_x_p, vort_y_p = (physical[2], physical[3])
    buoy_x_p, buoy_y_p = (physical[4], physical[5])
    advect_vort = (
        base_all[0] * vort_x_p
        + base_all[1] * vort_y_p
        + flow_x_p * base_all[2]
        + flow_y_p * base_all[3]
    )
    advect_buoy = (
        base_all[0] * buoy_x_p
        + base_all[1] * buoy_y_p
        + flow_x_p * base_all[4]
        + flow_y_p * base_all[5]
    )
    advect_both = jnp.stack([advect_vort, advect_buoy])
    y_forward = jnp.stack([cosine_table, -sine_table], axis=1)
    x_forward = jnp.stack(
        [
            jnp.concatenate([cosine_table, -sine_table], axis=1),
            jnp.concatenate([sine_table, cosine_table], axis=1),
        ]
    )
    spread = jnp.einsum(
        "fplxy,yck->fplckx", advect_both, y_forward, precision=lax.Precision.HIGHEST
    )
    spectra = jnp.einsum(
        "fplckx,cxm->fplkm",
        lax.all_to_all(spread, "pen", split_axis=4, concat_axis=5, tiled=True),
        x_forward,
        precision=lax.Precision.HIGHEST,
    )
    advect = (
        spectra[0][..., :grid_size],
        spectra[0][..., grid_size:],
        spectra[1][..., :grid_size],
        spectra[1][..., grid_size:],
    )
    tend = tendency(vort, buoy, advect, flow_y, kappa_x, square, 1)
    accum_next = memory_factor * accum + tend
    state_next = state + weight_factor * time_step * accum_next
    return (state_next, accum_next)


def solution(mesh):
    return jax.shard_map(
        on_device,
        mesh=mesh,
        in_specs=(
            P(None, "ens", None, "pen", None),
            P(None, "ens", None, "pen", None),
            P(None, None, "pen", "ens"),
        ),
        out_specs=(P(None, "ens", None, "pen", None), P(None, "ens", None, "pen", None)),
        check_vma=False,
    )
```

profile of v0, /device:TPU:1, one launch (start us, length us, event | category | flops | bytes accessed | tf_op | source)
XLA Modules:
  0.0 172.0 jit_solution(4518188159568962184)
XLA Ops:
  0.7 1.1 sine_multiply_fusion.1
  1.7 1.0 fusion.39
  2.7 0.0 copy-start.1
  2.7 1.1 slice_bitcast_fusion.1
  3.8 0.0 copy-start.4
  3.8 0.1 fusion.81
  3.9 0.6 copy-done.4
  4.5 0.7 fusion.97
  5.2 0.7 fusion.73
  6.0 0.0 copy-done.9
  6.0 0.0 copy-done.11
  6.0 0.5 copy-done.5
  6.5 0.0 copy-done.7
  6.5 0.0 copy-done.1
  6.5 1.5 convolution_bitcast_fusion
  8.0 5.0 %copy.20 = f32[6,1,4,2,256,16]{5,2,0,3,1,4:T(4,128)} copy(f32[6,1,4,2,256,16]{4,5,2,0,3,1:T(8,128)S(1)} %convolution_bitcast_fusion) | data formatting | bytes 1572864 | tf_op jit(solution)/shard_map/fplkj,jcx->fplcxk/transpose | solution.py:82
  13.0 7.2 %reshape.338 = f32[16,1,12288]{2,1,0:T(1,128)} reshape(f32[256,1,2,6,4,16]{5,4,3,2,1,0:T(4,128)} %bitcast.114) | data formatting | bytes 1572864
  20.2 10.2 %all-to-all-start = ((f32[16,1,12288]{2,1,0:T(1,128)}), f32[16,1,12288]{2,1,0:T(1,128)S(1)}, u32[]{:S(2)}, u32[]{:S(2)}) async-start(f32[16,1,12288]{2,1,0:T(1,128)} %reshape.338), calls=%async_computation | async-start | bytes 1572864 | tf_op jit(solution)/shard_map/all_to_all | solution.py:87
  30.4 0.0 copy-done.22
  30.5 71.0 %all_gather.3 = f32[6,4,16,256]{2,1,0,3:T(4,128)S(1)} all-gather(f32[6,4,16,8]{2,1,0,3:T(4,128)S(1)} %copy.13), channel_id=1, replica_groups=mesh['ens'=32,'pen'=16] {'ens'}, dimensions={3}, use_global_device_ids=true | all-gather | bytes 405504 | tf_op jit(solution)/shard_map/all_gather | solution.py:96
  101.4 1.5 fusion.94
  102.9 1.8 %copy.35 = f32[1,4,16,256]{3,2,1,0:T(8,128)} copy(f32[1,4,16,256]{2,1,0,3:T(4,128)} %get-tuple-element.8) | data formatting | bytes 131072
  104.8 1.8 %copy.36 = f32[1,4,16,256]{3,2,1,0:T(8,128)} copy(f32[1,4,16,256]{2,1,0,3:T(4,128)} %get-tuple-element.7) | data formatting | bytes 131072
  106.6 0.8 copy.37
  107.4 0.8 copy.38
  108.2 0.2 copy.39
  108.4 0.2 copy.40
  108.6 1.7 fusion.40
  110.3 1.1 multiply_negate_fusion
  111.4 0.0 all-to-all-done
  111.4 0.5 broadcast.510
  111.9 2.4 %reduce = f32[16,12288]{1,0:T(8,128)S(1)} reduce(f32[16,1,12288]{2,1,0:T(1,128)S(1)} %all-to-all-done, f32[]{:T(128)} %broadcast.510), dimensions={1}, to_apply=%all_to_all.22.reduce_sub_computation | reduce | bytes 1572868 | tf_op jit(solution)/shard_map/all_to_all | solution.py:87
  114.3 6.3 %reshape.339 = f32[256,1,2,6,4,16]{5,4,3,2,1,0:T(4,128)} reshape(f32[16,12288]{1,0:T(8,128)S(1)} %reduce) | data formatting | bytes 1572864
  120.6 9.1 %copy.43 = f32[6,1,4,2,16,16,16]{6,4,5,3,2,0,1:T(8,128)} copy(f32[6,1,4,2,16,16,16]{6,2,0,3,5,4,1:T(4,128)} %bitcast.115) | data formatting | bytes 1572864 | tf_op jit(solution)/shard_map/all_to_all | solution.py:87
  129.7 0.0 copy-start.2
  129.7 4.9 %reshape.327 = f32[6,4,2,16,256]{4,3,2,1,0:T(8,128)S(1)} reshape(f32[6,1,4,2,16,16,16]{6,5,4,3,2,0,1:T(8,128)} %bitcast.116) | data formatting | bytes 1572864 | tf_op jit(solution)/shard_map/reshape.16
  134.7 0.8 convolution_bitcast_fusion.1
  135.5 0.0 copy-done.13
  135.5 0.0 copy-done.14
  135.5 0.0 copy-done.15
  135.5 0.0 copy-done.16
  135.5 0.1 fusion.72
  135.6 0.0 copy-done.2
  135.6 0.4 convolution_bitcast_fusion.2
  136.0 0.0 copy-start.3
  136.0 1.3 copy.27
  137.3 2.3 %reshape.340 = f32[16,1,4096]{2,1,0:T(1,128)} reshape(f32[256,1,2,2,4,16]{5,4,3,2,1,0:T(4,128)S(1)} %bitcast.117) | data formatting | bytes 524288
  139.6 9.8 %all-to-all-start.1 = ((f32[16,1,4096]{2,1,0:T(1,128)}), f32[16,1,4096]{2,1,0:T(1,128)S(1)}, u32[]{:S(2)}, u32[]{:S(2)}) async-start(f32[16,1,4096]{2,1,0:T(1,128)} %reshape.340), calls=%async_computation.1 | async-start | bytes 524288 | tf_op jit(solution)/shard_map/all_to_all | solution.py:157
  149.4 1.1 sine_multiply_fusion
  150.4 0.0 copy-done.3
  150.4 0.1 maximum_bitcast_fusion.8
  150.6 1.4 fusion.95
  152.0 10.0 %all-to-all-done.1 = f32[16,1,4096]{2,1,0:T(1,128)S(1)} async-done(((f32[16,1,4096]{2,1,0:T(1,128)}), f32[16,1,4096]{2,1,0:T(1,128)S(1)}, u32[]{:S(2)}, u32[]{:S(2)}) %all-to-all-start.1) | async-done | bytes 262176 | tf_op jit(solution)/shard_map/all_to_all | solution.py:157
  162.0 1.2 reduce.1
  163.2 1.5 reshape.341
  164.8 2.6 %copy.44 = f32[2,1,4,2,16,16,16]{6,4,5,3,2,0,1:T(8,128)} copy(f32[2,1,4,2,16,16,16]{6,2,0,3,5,4,1:T(4,128)S(1)} %bitcast.118) | data formatting | bytes 524288 | tf_op jit(solution)/shard_map/all_to_all | solution.py:157
  167.4 0.0 copy-start.23
  167.4 0.0 copy-start
  167.4 0.0 copy-start.17
  167.4 2.6 %reshape.329 = f32[2,4,2,16,256]{4,3,2,1,0:T(8,128)S(1)} reshape(f32[2,1,4,2,16,16,16]{6,5,4,3,2,0,1:T(8,128)} %bitcast.119) | data formatting | bytes 524288 | tf_op jit(solution)/shard_map/reshape.33
  170.0 0.7 convolution_bitcast_fusion.3
  170.8 0.1 fusion.56
  171.0 0.1 fusion.62
  171.1 0.9 multiply_add_fusion
  (55 shorter events, 0.2 us)
Async XLA Ops:
  2.7 3.8 %copy-start.1 = (f32[256,1,256]{2,0,1:T(8,128)}, f32[256,1,256]{2,0,1:T(8,128)S(1)}, u32[]{:S(2)}) copy-start(f32[256,1,256]{2,0,1:T(8,128)S(1)} %fusion.39) | copy-start | bytes 786436
  3.8 0.7 copy-start.4
  5.1 0.8 copy-start.9
  5.1 0.8 copy-start.11
  5.9 0.6 copy-start.5
  5.9 0.7 copy-start.7
  13.0 17.4 %copy-start.22 = (f32[6,4,16,8]{2,3,1,0:T(8,128)S(1)}, f32[6,4,16,8]{2,3,1,0:T(8,128)}, u32[]{:S(2)}) copy-start(f32[6,4,16,8]{2,3,1,0:T(8,128)} %param.5) | copy-start | bytes 36868
  20.2 91.2 %all-to-all-start = ((f32[16,1,12288]{2,1,0:T(1,128)}), f32[16,1,12288]{2,1,0:T(1,128)S(1)}, u32[]{:S(2)}, u32[]{:S(2)}) async-start(f32[16,1,12288]{2,1,0:T(1,128)} %reshape.338), calls=%async_computation | async-start | bytes 1572864 | tf_op jit(solution)/shard_map/all_to_all | solution.py:87
  129.7 5.8 %copy-start.13 = (f32[1,4,16,256]{3,2,1,0:T(8,128)S(1)}, f32[1,4,16,256]{3,2,1,0:T(8,128)}, u32[]{:S(2)}) copy-start(f32[1,4,16,256]{3,2,1,0:T(8,128)} %copy.35) | copy-start | bytes 196612
  129.7 5.8 %copy-start.14 = (f32[1,4,16,256]{3,2,1,0:T(8,128)S(1)}, f32[1,4,16,256]{3,2,1,0:T(8,128)}, u32[]{:S(2)}) copy-start(f32[1,4,16,256]{3,2,1,0:T(8,128)} %copy.36) | copy-start | bytes 196612
  129.7 5.8 %copy-start.15 = (f32[1,4,16,256]{3,2,1,0:T(8,128)S(1)}, f32[1,4,16,256]{3,2,1,0:T(8,128)}, u32[]{:S(2)}) copy-start(f32[1,4,16,256]{3,2,1,0:T(8,128)} %copy.37) | copy-start | bytes 196612
  129.7 5.8 %copy-start.16 = (f32[1,4,16,256]{3,2,1,0:T(8,128)S(1)}, f32[1,4,16,256]{3,2,1,0:T(8,128)}, u32[]{:S(2)}) copy-start(f32[1,4,16,256]{3,2,1,0:T(8,128)} %copy.38) | copy-start | bytes 196612
  129.7 5.9 %copy-start.2 = (f32[256,1,256]{2,0,1:T(8,128)S(1)}, f32[256,1,256]{2,0,1:T(8,128)}, u32[]{:S(2)}) copy-start(f32[256,1,256]{2,0,1:T(8,128)} %copy-done.1) | copy-start | bytes 786436
  136.0 14.4 %copy-start.3 = (f32[256,256]{1,0:T(8,128)S(1)}, f32[256,256]{1,0:T(8,128)}, u32[]{:S(2)}) copy-start(f32[256,256]{1,0:T(8,128)} %fusion.40) | copy-start | bytes 786436
  139.6 22.4 %all-to-all-start.1 = ((f32[16,1,4096]{2,1,0:T(1,128)}), f32[16,1,4096]{2,1,0:T(1,128)S(1)}, u32[]{:S(2)}, u32[]{:S(2)}) async-start(f32[16,1,4096]{2,1,0:T(1,128)} %reshape.340), calls=%async_computation.1 | async-start | bytes 524288 | tf_op jit(solution)/shard_map/all_to_all | solution.py:157
  164.7 6.0 %copy-start.8 = (f32[1,4,16,256]{3,2,1,0:T(8,128)S(1)}, f32[1,4,16,256]{3,2,1,0:T(8,128)}, u32[]{:S(2)}) copy-start(f32[1,4,16,256]{3,2,1,0:T(8,128)} %copy-done.7) | copy-start | bytes 196612
  164.7 6.0 %copy-start.12 = (f32[1,4,16,256]{3,2,1,0:T(8,128)S(1)}, f32[1,4,16,256]{3,2,1,0:T(8,128)}, u32[]{:S(2)}) copy-start(f32[1,4,16,256]{3,2,1,0:T(8,128)} %copy-done.11) | copy-start | bytes 196612
  164.7 6.0 %copy-start.19 = (f32[1,4,16,256]{3,2,1,0:T(8,128)S(1)}, f32[1,4,16,256]{3,2,1,0:T(8,128)}, u32[]{:S(2)}) copy-start(f32[1,4,16,256]{3,2,1,0:T(8,128)} %get-tuple-element.29) | copy-start | bytes 196612
  164.7 6.0 %copy-start.21 = (f32[1,4,16,256]{3,2,1,0:T(8,128)S(1)}, f32[1,4,16,256]{3,2,1,0:T(8,128)}, u32[]{:S(2)}) copy-start(f32[1,4,16,256]{3,2,1,0:T(8,128)} %get-tuple-element.38) | copy-start | bytes 196612
  164.8 6.0 %copy-start.27 = (f32[1,1,16,256]{3,2,1,0:T(8,128)S(1)}, f32[1,1,16,256]{3,2,1,0:T(8,128)}, u32[]{:S(2)}) copy-start(f32[1,1,16,256]{3,2,1,0:T(8,128)} %get-tuple-element.31) | copy-start | bytes 49156
  164.8 6.0 %copy-start.28 = (f32[1,1,16,256]{3,2,1,0:T(8,128)S(1)}, f32[1,1,16,256]{3,2,1,0:T(8,128)}, u32[]{:S(2)}) copy-start(f32[1,1,16,256]{3,2,1,0:T(8,128)} %get-tuple-element.32) | copy-start | bytes 49156
  164.8 6.0 %copy-start.29 = (f32[1,1,16,256]{3,2,1,0:T(8,128)S(1)}, f32[1,1,16,256]{3,2,1,0:T(8,128)}, u32[]{:S(2)}) copy-start(f32[1,1,16,256]{3,2,1,0:T(8,128)} %get-tuple-element.48) | copy-start | bytes 49156
  164.8 6.0 %copy-start.30 = (f32[1,1,16,256]{3,2,1,0:T(8,128)S(1)}, f32[1,1,16,256]{3,2,1,0:T(8,128)}, u32[]{:S(2)}) copy-start(f32[1,1,16,256]{3,2,1,0:T(8,128)} %get-tuple-element.51) | copy-start | bytes 49156
  167.4 3.5 %copy-start.6 = (f32[1,4,16,256]{3,2,1,0:T(8,128)S(1)}, f32[1,4,16,256]{3,2,1,0:T(8,128)}, u32[]{:S(2)}) copy-start(f32[1,4,16,256]{3,2,1,0:T(8,128)} %copy-done.5) | copy-start | bytes 196612
  167.4 3.5 %copy-start.10 = (f32[1,4,16,256]{3,2,1,0:T(8,128)S(1)}, f32[1,4,16,256]{3,2,1,0:T(8,128)}, u32[]{:S(2)}) copy-start(f32[1,4,16,256]{3,2,1,0:T(8,128)} %copy-done.9) | copy-start | bytes 196612
  167.4 3.5 %copy-start.18 = (f32[1,4,16,256]{3,2,1,0:T(8,128)S(1)}, f32[1,4,16,256]{3,2,1,0:T(8,128)}, u32[]{:S(2)}) copy-start(f32[1,4,16,256]{3,2,1,0:T(8,128)} %get-tuple-element.28) | copy-start | bytes 196612
  167.4 3.5 %copy-start.20 = (f32[1,4,16,256]{3,2,1,0:T(8,128)S(1)}, f32[1,4,16,256]{3,2,1,0:T(8,128)}, u32[]{:S(2)}) copy-start(f32[1,4,16,256]{3,2,1,0:T(8,128)} %get-tuple-element.43) | copy-start | bytes 196612
  167.4 3.6 %copy-start.23 = (f32[1,1,16,256]{3,2,1,0:T(8,128)S(1)}, f32[1,1,16,256]{3,2,1,0:T(8,128)}, u32[]{:S(2)}) copy-start(f32[1,1,16,256]{3,2,1,0:T(8,128)} %get-tuple-element.30) | copy-start | bytes 49156
  167.4 3.6 %copy-start.24 = (f32[1,1,16,256]{3,2,1,0:T(8,128)S(1)}, f32[1,1,16,256]{3,2,1,0:T(8,128)}, u32[]{:S(2)}) copy-start(f32[1,1,16,256]{3,2,1,0:T(8,128)} %get-tuple-element.33) | copy-start | bytes 49156
  167.4 3.6 %copy-start.25 = (f32[1,1,16,256]{3,2,1,0:T(8,128)S(1)}, f32[1,1,16,256]{3,2,1,0:T(8,128)}, u32[]{:S(2)}) copy-start(f32[1,1,16,256]{3,2,1,0:T(8,128)} %get-tuple-element.49) | copy-start | bytes 49156
  167.4 3.6 %copy-start.26 = (f32[1,1,16,256]{3,2,1,0:T(8,128)S(1)}, f32[1,1,16,256]{3,2,1,0:T(8,128)}, u32[]{:S(2)}) copy-start(f32[1,1,16,256]{3,2,1,0:T(8,128)} %get-tuple-element.50) | copy-start | bytes 49156
  167.4 3.6 %copy-start = (f32[2,1,4,16,512]{4,3,2,1,0:T(8,128)S(1)}, f32[2,1,4,16,512]{4,3,2,1,0:T(8,128)}, u32[]{:S(2)}) copy-start(f32[2,1,4,16,512]{4,3,2,1,0:T(8,128)} %param.3) | copy-start | bytes 786436
  167.4 3.6 %copy-start.17 = (f32[2,1,4,16,512]{4,3,2,1,0:T(8,128)S(1)}, f32[2,1,4,16,512]{4,3,2,1,0:T(8,128)}, u32[]{:S(2)}) copy-start(f32[2,1,4,16,512]{4,3,2,1,0:T(8,128)} %param.4) | copy-start | bytes 786436
where the time goes:
time: 173 us; the launch traced here: 172 us
  blocking collectives  71 us (41%)
  local copies, waits for them, and re-layouts  54.2 us (31%)
  starting transfers between devices  20 us (12%)
  other arithmetic  12.2 us (7%)
  waiting for transfers between devices  10 us (6%)
  matrix products  3.41 us (2%)
    all_gather x1, blocking collectives, on_device(): base_all = lax.all_gather(base_flow, 'ens', axis=3, tiled=True)  71 us
    unnamed x73, local copies, waits for them, and re-layouts  24.2 us
    all_to_all x1, starting transfers between devices, to_physical(): lax.all_to_all(mixed_space, 'pen', split_axis=4, concat_axis=5, tiled=True)  10.2 us
    all_to_all x1, waiting for transfers between devices, on_device(): lax.all_to_all(spread, 'pen', split_axis=4, concat_axis=5, tiled=True)  10 us
    all_to_all x1, starting transfers between devices, on_device(): lax.all_to_all(spread, 'pen', split_axis=4, concat_axis=5, tiled=True)  9.75 us
    all_to_all x2, local copies, waits for them, and re-layouts, to_physical(): lax.all_to_all(mixed_space, 'pen', split_axis=4, concat_axis=5, tiled=True)  9.59 us
    another operation x2, local copies, waits for them, and re-layouts  7.5 us
    transpose x1, local copies, waits for them, and re-layouts, to_physical(): jnp.einsum('fplkj,jcx->fplcxk', spectral, x_table, precision=lax.Precisio...  4.97 us
  transfers between devices with their start and end apart: 2, of which 1 were waited for; matrix products, arithmetic and copies ran while one was open for 7% of the time, Pallas kernels for 0%

commit v1 on v0

v1 whole, which is shorter than its diff:
```python
import functools
import math

import jax
import jax.numpy as jnp
import numpy as np
from jax import lax
from jax.experimental import pallas as pl
from jax.experimental.pallas import tpu as pltpu
from jax.sharding import PartitionSpec as P

viscosity = 0.05
vertical_mixing = 0.5
buoyancy_gain = 0.5
stratification = 0.5
memory_factor = -5.0 / 9.0
weight_factor = 15.0 / 16.0
time_step = 0.4

GRID = 256
LEVELS = 4
ROWS = 16
PEN = 16
CHUNK = 64
MESH = pl.DeviceIdType.MESH
F32 = jnp.float32
BF16 = jnp.bfloat16


def halves(table):
    high = table.astype(np.float32).astype(jnp.bfloat16)
    low = (table - high.astype(np.float64)).astype(np.float32).astype(jnp.bfloat16)
    return np.stack([high, low])


def tables():
    position = np.arange(GRID)
    angle = 2.0 * np.pi / GRID * (position[:, None] * position[None, :] % GRID)
    cosine, sine = np.cos(angle) / 16.0, np.sin(angle) / 16.0
    x_inverse = np.stack([np.stack([cosine, sine], 1), np.stack([-sine, cosine], 1)])
    x_inverse = x_inverse.reshape(2, GRID, 2, GRID // CHUNK, CHUNK).transpose(0, 1, 3, 2, 4)
    x_inverse = x_inverse.reshape(2 * GRID, 2 * GRID)
    y_table = np.concatenate([cosine, sine])
    return halves(x_inverse), halves(y_table), halves(x_inverse.T.copy())


def split(value):
    high = value.astype(BF16)
    return high, (value - high.astype(F32)).astype(BF16)


def dot(a, b):
    return jnp.dot(a, b, preferred_element_type=F32)


def product(a, b):
    return dot(a[0], b[0]) + (dot(a[1], b[0]) + dot(a[0], b[1]))


def exact(a, b, dims):
    return lax.dot_general(
        a, b, (dims, ((), ())), precision=lax.Precision.HIGHEST, preferred_element_type=F32
    )


def wave_numbers(shape, dim, offset):
    position = lax.broadcasted_iota(jnp.int32, shape, dim) + offset
    signed = jnp.where(position <= GRID // 2, position, position - GRID)
    derivative = jnp.where(position == GRID // 2, 0, signed)
    return (2.0 * math.pi / GRID) * derivative.astype(F32), signed


def kernel(
    groups,
    state_hbm, accum_hbm, base_hbm, xt_hbm, yt_hbm, xf_hbm,
    state_next, accum_next,
    st, ac, bs, xt, yt, xf, xs, g, b0, b1, bb, ys, h, lin,
    load_sem, out_sem, fs, fr, rs, rr, as_, ar, cs, cr, hs, hr, own_sem,
):
    ens = lax.axis_index("ens")
    pen = lax.axis_index("pen")
    pair, core = ens // 2, ens % 2
    column, row = pen // 4, pen % 4
    other = ens + 1 - 2 * core
    rows_y = GRID // (2 * groups)

    barrier = pltpu.get_barrier_semaphore()
    for k in range(1, PEN):
        pl.semaphore_signal(barrier, inc=1, device_id=(ens, (pen + k) % PEN), device_id_type=MESH)
    for k in range(1, groups):
        pl.semaphore_signal(
            barrier, inc=1, device_id=((pair + k) % groups * 2 + core, pen), device_id_type=MESH
        )
    pl.semaphore_signal(barrier, inc=1, device_id=(other, pen), device_id_type=MESH)

    loads = [
        pltpu.make_async_copy(source, target, load_sem.at[i])
        for i, (source, target) in enumerate(
            [(base_hbm, bs), (state_hbm, st), (xt_hbm, xt), (accum_hbm, ac), (yt_hbm, yt), (xf_hbm, xf)]
        )
    ]
    for load in loads:
        load.start()

    loads[0].wait()
    unit = (
        lax.broadcasted_iota(jnp.int32, (rows_y, rows_y), 0)
        == lax.broadcasted_iota(jnp.int32, (rows_y, rows_y), 1)
    ).astype(F32)
    source_lane = lax.broadcasted_iota(jnp.int32, (96, 384), 0)
    place = (
        lax.broadcasted_iota(jnp.int32, (96, 384), 1)
        == source_lane // 16 * CHUNK + source_lane % 16 + row * 16
    ).astype(F32)
    for level in range(LEVELS):
        turned = exact(unit, bs[:, level].reshape(96, rows_y), ((1,), (1,)))
        b0[level] = exact(turned, place, ((1,), (0,)))

    kappa_y, signed_y = wave_numbers((ROWS, 1), 0, pen * ROWS)
    kappa_x, signed_x = wave_numbers((1, GRID), 1, 0)
    wave_square = signed_y * signed_y + signed_x * signed_x
    factor = (2.0 * math.pi / GRID) ** 2
    square = factor * wave_square.astype(F32)
    inverse = jnp.where(
        wave_square > 0, 1.0 / (factor * jnp.maximum(wave_square, 1).astype(F32)), 0.0
    )

    loads[1].wait()
    loads[2].wait()

    def transform_x(level):
        zr, zi = st[0, level, :, :GRID], st[0, level, :, GRID:]
        tr, ti = st[1, level, :, :GRID], st[1, level, :, GRID:]
        wzr, wzi = kappa_x * zr - kappa_y * zi, kappa_x * zi + kappa_y * zr
        wtr, wti = kappa_x * tr - kappa_y * ti, kappa_x * ti + kappa_y * tr
        packed = jnp.concatenate(
            [
                jnp.concatenate([wzr * inverse, wzi * inverse], axis=1),
                jnp.concatenate([-wzi, wzr], axis=1),
                jnp.concatenate([-wti, wtr], axis=1),
            ],
            axis=0,
        )
        mixed = product(split(packed), (xt[0], xt[1]))
        for c in range(4):
            xs[level, c] = mixed[:, 128 * c : 128 * (c + 1)].reshape(3, ROWS, 128)

    def forward(level, c):
        target = c * 4 + level
        return pltpu.make_async_remote_copy(
            src_ref=xs.at[level, c],
            dst_ref=g.at[pen],
            send_sem=fs.at[target],
            recv_sem=fr.at[pen],
            device_id=(ens, target),
            device_id_type=MESH,
        )

    def spread(k):
        target = column * 4 + (row + k) % 4
        return pltpu.make_async_remote_copy(
            src_ref=b0.at[(row + k) % 4],
            dst_ref=b1.at[row],
            send_sem=as_.at[(row + k) % 4],
            recv_sem=ar.at[row],
            device_id=(ens, target),
            device_id_type=MESH,
        )

    transform_x((row + 2) % 4)
    pl.semaphore_wait(barrier, PEN - 1 + groups - 1 + 1)
    for k in (2, 1, 3):
        spread(k).start()
    for step, k in enumerate((2, 1, 3, 0)):
        level = (row + k) % 4
        if step > 0:
            transform_x(level)
        for m in (2, 1, 3, 0):
            if k != 0 or m != 0:
                forward(level, (column + m) % 4).start()
    own = pltpu.make_async_copy(xs.at[row, column], g.at[pen], own_sem.at[0])
    own.start()

    def gather(k):
        target = (pair + k) % groups
        return pltpu.make_async_remote_copy(
            src_ref=bb.at[pair, core],
            dst_ref=bb.at[pair, core],
            send_sem=hs.at[target],
            recv_sem=hr.at[pair],
            device_id=(target * 2 + core, pen),
            device_id_type=MESH,
        )

    def gathered(k):
        source = (pair + k) % groups
        return pltpu.make_async_remote_copy(
            src_ref=bb.at[source, core],
            dst_ref=bb.at[source, core],
            send_sem=hs.at[source],
            recv_sem=hr.at[source],
            device_id=(source * 2 + core, pen),
            device_id_type=MESH,
        )

    def spread_from(k):
        source = (row + k) % 4
        return pltpu.make_async_remote_copy(
            src_ref=b0.at[source],
            dst_ref=b1.at[source],
            send_sem=as_.at[source],
            recv_sem=ar.at[source],
            device_id=(ens, column * 4 + source),
            device_id_type=MESH,
        )

    b1[row] = b0[row]
    for k in range(1, 4):
        spread_from(k).wait_recv()
    bb[pair, core] = (b1[0] + b1[1]) + (b1[2] + b1[3])
    for k in range(1, groups):
        gather(k).start()

    loads[3].wait()
    for level in range(LEVELS):
        up, down = min(level + 1, LEVELS - 1), max(level - 1, 0)
        zr, zi = st[0, level, :, :GRID], st[0, level, :, GRID:]
        tr, ti = st[1, level, :, :GRID], st[1, level, :, GRID:]
        across = stratification * kappa_x * inverse
        linear = (
            jnp.concatenate([-buoyancy_gain * kappa_x * ti, buoyancy_gain * kappa_x * tr], axis=1),
            jnp.concatenate([-across * zi, across * zr], axis=1),
        )
        damping = viscosity * jnp.concatenate([square, square], axis=1)
        for field in range(2):
            value = st[field, level]
            mixing = st[field, up] + st[field, down] - 2.0 * value
            lin[field, level] = (
                memory_factor * ac[field, level]
                + linear[field]
                - damping * value
                + vertical_mixing * mixing
            )

    for k in range(1, groups):
        gathered(k).wait_recv()
    swap = pltpu.make_async_remote_copy(
        src_ref=bb.at[:, core],
        dst_ref=bb.at[:, core],
        send_sem=cs.at[0],
        recv_sem=cr.at[0],
        device_id=(other, pen),
        device_id_type=MESH,
    )
    swap.start()

    loads[4].wait()
    own.wait()

    def forward_from(k):
        source = (pen + k) % PEN
        return pltpu.make_async_remote_copy(
            src_ref=xs.at[source % 4, source // 4],
            dst_ref=g.at[source],
            send_sem=fs.at[source],
            recv_sem=fr.at[source],
            device_id=(ens, source),
            device_id_type=MESH,
        )

    for k in range(1, PEN):
        forward_from(k).wait_recv()

    table = (yt[0], yt[1])
    spectral = jnp.concatenate([g[:, f].reshape(GRID, 128) for f in range(3)], axis=1)
    turned = product(table, split(spectral))
    lane = lax.broadcasted_iota(jnp.int32, (1, 128), 1)
    first = lane < CHUNK
    sign = jnp.where(first, -1.0, 1.0)

    def swap_halves(value):
        return pltpu.roll(value, CHUNK, 1)

    physical = []
    for f in range(3):
        even = turned[:GRID, 128 * f : 128 * (f + 1)]
        odd = turned[GRID:, 128 * f : 128 * (f + 1)]
        physical.append(even + sign * swap_halves(odd))

    pltpu.make_async_remote_copy(
        src_ref=bb.at[:, 1 - core],
        dst_ref=bb.at[:, 1 - core],
        send_sem=cs.at[0],
        recv_sem=cr.at[0],
        device_id=(other, pen),
        device_id_type=MESH,
    ).wait_recv()
    base = bb[...].reshape(GRID, 384)
    flow, vort_slope, buoy_slope = base[:, :128], base[:, 128:256], base[:, 256:]
    advect_vort = flow * physical[1] + vort_slope * physical[0]
    advect_buoy = flow * physical[2] + buoy_slope * physical[0]
    advect = jnp.where(
        first, advect_vort + swap_halves(advect_vort), advect_buoy + swap_halves(advect_buoy)
    )
    spread_y = product(table, split(advect))
    real, imag = spread_y[:GRID], -spread_y[GRID:]
    ys[:, 0] = jnp.where(first, real, swap_halves(imag)).reshape(PEN, ROWS, 128)
    ys[:, 1] = jnp.where(first, swap_halves(real), imag).reshape(PEN, ROWS, 128)

    def backward(target):
        return pltpu.make_async_remote_copy(
            src_ref=ys.at[target],
            dst_ref=h.at[pen],
            send_sem=rs.at[target],
            recv_sem=rr.at[pen],
            device_id=(ens, target),
            device_id_type=MESH,
        )

    def backward_from(source):
        return pltpu.make_async_remote_copy(
            src_ref=ys.at[source],
            dst_ref=h.at[source],
            send_sem=rs.at[source],
            recv_sem=rr.at[source],
            device_id=(ens, source),
            device_id_type=MESH,
        )

    for k in (2, 1, 3, 0):
        for m in (2, 1, 3, 0):
            if k != 0 or m != 0:
                backward((column + m) % 4 * 4 + (row + k) % 4).start()
    h[pen] = ys[pen]
    loads[5].wait()
    for k in range(1, PEN):
        backward_from((pen + k) % PEN).wait_recv()

    gathered_x = jnp.concatenate([h[4 * c : 4 * c + 4].reshape(128, 128) for c in range(4)], axis=1)
    spectra = product(split(gathered_x), (xf[0], xf[1]))
    step = weight_factor * time_step
    for level in range(LEVELS):
        for field in range(2):
            start = (level * 2 + field) * ROWS
            value = lin[field, level] - spectra[start : start + ROWS]
            lin[field, level] = value
            st[field, level] = st[field, level] + step * value
    outs = [
        pltpu.make_async_copy(lin, accum_next, out_sem.at[0]),
        pltpu.make_async_copy(st, state_next, out_sem.at[1]),
    ]
    for out in outs:
        out.start()

    for k in (1, 2, 3):
        spread_from(k).wait_send()
    for k in range(1, groups):
        gathered(k).wait_send()
    swap.wait_send()
    for k in range(1, PEN):
        forward_from(k).wait_send()
        backward_from((pen + k) % PEN).wait_send()
    for out in outs:
        out.wait()


def on_device(groups, state, accum, base_flow):
    rows_y = GRID // (2 * groups)
    x_inverse, y_table, x_forward = tables()
    fields = (2, LEVELS, ROWS, 2 * GRID)
    result = jax.ShapeDtypeStruct(fields, F32)
    dma = pltpu.SemaphoreType.DMA
    outputs = pl.pallas_call(
        functools.partial(kernel, groups),
        out_shape=(result, result),
        in_specs=[pl.BlockSpec(memory_space=pl.ANY)] * 6,
        out_specs=(pl.BlockSpec(memory_space=pl.ANY),) * 2,
        scratch_shapes=[
            pltpu.VMEM(fields, F32),
            pltpu.VMEM(fields, F32),
            pltpu.VMEM((6, LEVELS, 16, rows_y), F32),
            pltpu.VMEM((2, 2 * GRID, 2 * GRID), BF16),
            pltpu.VMEM((2, 2 * GRID, GRID), BF16),
            pltpu.VMEM((2, 2 * GRID, 2 * GRID), BF16),
            pltpu.VMEM((LEVELS, 4, 3, ROWS, 128), F32),
            pltpu.VMEM((PEN, 3, ROWS, 128), F32),
            pltpu.VMEM((LEVELS, rows_y, 384), F32),
            pltpu.VMEM((4, rows_y, 384), F32),
            pltpu.VMEM((groups, 2, rows_y, 384), F32),
            pltpu.VMEM((PEN, 2, ROWS, 128), F32),
            pltpu.VMEM((PEN, 2, ROWS, 128), F32),
            pltpu.VMEM(fields, F32),
            dma((6,)),
            dma((2,)),
            dma((PEN,)),
            dma((PEN,)),
            dma((PEN,)),
            dma((PEN,)),
            dma((4,)),
            dma((4,)),
            dma((1,)),
            dma((1,)),
            dma((groups,)),
            dma((groups,)),
            dma((1,)),
        ],
        compiler_params=pltpu.CompilerParams(
            collective_id=0, has_side_effects=True, vmem_limit_bytes=40 * 1024 * 1024
        ),
        name="step",
    )(
        state.reshape(fields), accum.reshape(fields), base_flow,
        jnp.asarray(x_inverse), jnp.asarray(y_table), jnp.asarray(x_forward),
    )
    return tuple(out.reshape(state.shape) for out in outputs)


def solution(mesh):
    spectral = P(None, "ens", None, "pen", None)
    return jax.shard_map(
        functools.partial(on_device, mesh.shape["ens"] // 2),
        mesh=mesh,
        in_specs=(spectral, spectral, P(None, None, "pen", "ens")),
        out_specs=(spectral, spectral),
        check_vma=False,
    )
```

time: 173 us -> 49.8 us (0.29)
  blocking collectives: 71 us -> 0 us
  local copies, waits for them, and re-layouts: 54.2 us -> 6.89 us
  Pallas kernels: 0 us -> 41.9 us
  starting transfers between devices: 20 us -> 0 us
  other arithmetic: 12.2 us -> 0 us
  waiting for transfers between devices: 10 us -> 0 us
  matrix products: 3.41 us -> 0 us
    all_gather x1 -> x0, blocking collectives: 71 us -> none  [on_device(): base_all = lax.all_gather(base_flow, 'ens', axis=3, tiled=True)]
    pallas_call x0 -> x1, Pallas kernels: none -> 41.9 us  [on_device(): pl.pallas_call(functools.partial(kernel, groups), out_shape=(result, resu...]
    all_to_all x2 -> x0, starting transfers between devices: 20 us -> none  [the longest x1 10.2 us: to_physical(): lax.all_to_all(mixed_space, 'pen', split_axis=4, concat_axis=5, tiled=True)]
    unnamed x73 -> x13, local copies, waits for them, and re-layouts: 24.2 us -> 6.89 us
    all_to_all x3 -> x0, local copies, waits for them, and re-layouts: 12.2 us -> none  [the longest x2 9.59 us: to_physical(): lax.all_to_all(mixed_space, 'pen', split_axis=4, concat_axis=5, tiled=True)]
    all_to_all x2 -> x0, waiting for transfers between devices: 10 us -> none  [the longest x1 10 us: on_device(): lax.all_to_all(spread, 'pen', split_axis=4, concat_axis=5, tiled=True)]
    another operation x2 -> x0, local copies, waits for them, and re-layouts: 7.5 us -> none
    transpose x2 -> x0, local copies, waits for them, and re-layouts: 6.26 us -> none  [the longest x1 4.97 us: to_physical(): jnp.einsum('fplkj,jcx->fplcxk', spectral, x_table, precision=lax.Precisio...]
  transfers between devices with their start and end apart: 2 -> 0, of which waited for: 1 -> 0; matrix products, arithmetic and copies ran while one was open for 7% -> 0% of each run, Pallas kernels for 0% -> 0%
where the time goes in v1:
time: 49.8 us; the launch traced here: 49.5 us
  Pallas kernels  41.9 us (84%)
  local copies, waits for them, and re-layouts  6.89 us (14%)
  between operations  0.67 us (1%)
    pallas_call x1, Pallas kernels, on_device(): pl.pallas_call(functools.partial(kernel, groups), out_shape=(result, resu...  41.9 us
    unnamed x13, local copies, waits for them, and re-layouts  6.89 us

profile of v1, /device:TPU:1, one launch (start us, length us, event | category | flops | bytes accessed | tf_op | source)
XLA Modules:
  0.0 49.5 jit_solution(5322877006476454155)
XLA Ops:
  0.6 0.0 copy-start.3
  0.6 1.0 %copy.8.base_hbm = f32[6,4,16,8]{3,2,1,0:T(8,128)S(1)} copy(f32[6,4,16,8]{2,3,1,0:T(8,128)} %param.8) | data formatting | bytes 24576 | tf_op args[2]
  1.7 0.0 copy-done.3
  1.7 0.0 copy-start
  1.7 1.2 %copy-done = bf16[2,512,512]{2,1,0:T(8,128)(2,1)S(1)} copy-done((bf16[2,512,512]{2,1,0:T(8,128)(2,1)S(1)}, bf16[2,512,512]{2,1,0:T(8,128)(2,1)}, u32[]{:S(2)}) %copy-start) | copy-done | bytes 1048600
  2.9 0.0 copy-start.1
  2.9 1.2 %copy-done.1 = bf16[2,512,512]{2,1,0:T(8,128)(2,1)S(1)} copy-done((bf16[2,512,512]{2,1,0:T(8,128)(2,1)S(1)}, bf16[2,512,512]{2,1,0:T(8,128)(2,1)}, u32[]{:S(2)}) %copy-start.1) | copy-done | bytes 1048600
  4.2 0.0 copy-start.2
  4.2 1.0 %copy-done.2 = bf16[2,512,256]{2,1,0:T(8,128)(2,1)S(1)} copy-done((bf16[2,512,256]{2,1,0:T(8,128)(2,1)S(1)}, bf16[2,512,256]{2,1,0:T(8,128)(2,1)}, u32[]{:S(2)}) %copy-start.2) | copy-done | bytes 524312
  5.2 0.0 copy-start.4
  5.2 0.9 %copy-done.4 = f32[2,1,4,16,512]{4,3,2,1,0:T(8,128)S(1)} copy-done((f32[2,1,4,16,512]{4,3,2,1,0:T(8,128)S(1)}, f32[2,1,4,16,512]{4,3,2,1,0:T(8,128)}, u32[]{:S(2)}) %copy-start.4) | copy-done | bytes 262168
  6.1 41.9 %step.1 = (f32[2,4,16,512]{3,2,1,0:T(8,128)S(1)}, f32[2,4,16,512]{3,2,1,0:T(8,128)S(1)}) custom-call(f32[2,4,16,512]{3,2,1,0:T(8,128)S(1)} %bitcast.8, f32[2,4,16,512]{3,2,1,0:T(8,128)S(1)} %bitcast.9, f32[6,4,16,8]{3,2,1,0:T(8,128)S(1)} %copy.8.base_hbm, bf16[2,512,512]{2,1,0:T(8,128)(2,1)S(1)} %copy-done.1, bf16[2,512,256]{2,1,0:T(8,128)(2,1)S(1)} %copy-done.2, ...), custom_call_target="tpu_custom_call" | custom-call | tf_op jit(solution)/shard_map/step/pallas_call | solution.py:373
  48.1 0.7 %copy.13 = f32[2,1,4,16,512]{4,3,2,1,0:T(8,128)} copy(f32[2,1,4,16,512]{4,3,2,1,0:T(8,128)S(1)} %bitcast.11) | data formatting | bytes 524288
  48.8 0.7 %copy.14 = f32[2,1,4,16,512]{4,3,2,1,0:T(8,128)} copy(f32[2,1,4,16,512]{4,3,2,1,0:T(8,128)S(1)} %bitcast.10) | data formatting | bytes 524288
Async XLA Ops:
  0.6 1.1 %copy-start.3 = (f32[2,1,4,16,512]{4,3,2,1,0:T(8,128)S(1)}, f32[2,1,4,16,512]{4,3,2,1,0:T(8,128)}, u32[]{:S(2)}) copy-start(f32[2,1,4,16,512]{4,3,2,1,0:T(8,128)} %param.6) | copy-start | bytes 786436
  1.7 1.2 %copy-start = (bf16[2,512,512]{2,1,0:T(8,128)(2,1)S(1)}, bf16[2,512,512]{2,1,0:T(8,128)(2,1)}, u32[]{:S(2)}) copy-start(bf16[2,512,512]{2,1,0:T(8,128)(2,1)} %constant.8.clone.xf_hbm) | copy-start | bytes 3145732
  2.9 1.2 %copy-start.1 = (bf16[2,512,512]{2,1,0:T(8,128)(2,1)S(1)}, bf16[2,512,512]{2,1,0:T(8,128)(2,1)}, u32[]{:S(2)}) copy-start(bf16[2,512,512]{2,1,0:T(8,128)(2,1)} %constant.6.clone.xt_hbm) | copy-start | bytes 3145732
  4.2 1.0 %copy-start.2 = (bf16[2,512,256]{2,1,0:T(8,128)(2,1)S(1)}, bf16[2,512,256]{2,1,0:T(8,128)(2,1)}, u32[]{:S(2)}) copy-start(bf16[2,512,256]{2,1,0:T(8,128)(2,1)} %constant.7.clone.yt_hbm) | copy-start | bytes 1572868
  5.2 0.9 %copy-start.4 = (f32[2,1,4,16,512]{4,3,2,1,0:T(8,128)S(1)}, f32[2,1,4,16,512]{4,3,2,1,0:T(8,128)}, u32[]{:S(2)}) copy-start(f32[2,1,4,16,512]{4,3,2,1,0:T(8,128)} %param.7) | copy-start | bytes 786436

commit v2 on v1

--- a/solution.py
+++ b/solution.py
@@ -36,12 +36,9 @@
 def tables():
     position = np.arange(GRID)
     angle = 2.0 * np.pi / GRID * (position[:, None] * position[None, :] % GRID)
-    cosine, sine = np.cos(angle) / 16.0, np.sin(angle) / 16.0
-    x_inverse = np.stack([np.stack([cosine, sine], 1), np.stack([-sine, cosine], 1)])
-    x_inverse = x_inverse.reshape(2, GRID, 2, GRID // CHUNK, CHUNK).transpose(0, 1, 3, 2, 4)
-    x_inverse = x_inverse.reshape(2 * GRID, 2 * GRID)
-    y_table = np.concatenate([cosine, sine])
-    return halves(x_inverse), halves(y_table), halves(x_inverse.T.copy())
+    table = np.stack([np.cos(angle), np.sin(angle)], 1).reshape(GRID, 2, GRID // CHUNK, CHUNK)
+    table = table.transpose(0, 2, 1, 3).reshape(GRID, 2 * GRID) / 16.0
+    return halves(table), halves(table.T.copy())
 
 
 def split(value):
@@ -55,12 +52,6 @@
 
 def product(a, b):
     return dot(a[0], b[0]) + (dot(a[1], b[0]) + dot(a[0], b[1]))
-
-
-def exact(a, b, dims):
-    return lax.dot_general(
-        a, b, (dims, ((), ())), precision=lax.Precision.HIGHEST, preferred_element_type=F32
-    )
 
 
 def wave_numbers(shape, dim, offset):
@@ -72,10 +63,10 @@
 
 def kernel(
     groups,
-    state_hbm, accum_hbm, base_hbm, xt_hbm, yt_hbm, xf_hbm,
+    state_hbm, accum_hbm, base_hbm, wide_hbm, tall_hbm,
     state_next, accum_next,
-    st, ac, bs, xt, yt, xf, xs, g, b0, b1, bb, ys, h, lin,
-    load_sem, out_sem, fs, fr, rs, rr, as_, ar, cs, cr, hs, hr, own_sem,
+    st, ac, bs, wide, tall, xs, g, b0, b1, bb, ys, h, lin,
+    load_sem, fs, fr, rs, rr, as_, ar, cs, cr, hs, hr, own_sem,
 ):
     ens = lax.axis_index("ens")
     pen = lax.axis_index("pen")
@@ -96,25 +87,33 @@
     loads = [
         pltpu.make_async_copy(source, target, load_sem.at[i])
         for i, (source, target) in enumerate(
-            [(base_hbm, bs), (state_hbm, st), (xt_hbm, xt), (accum_hbm, ac), (yt_hbm, yt), (xf_hbm, xf)]
+            [(base_hbm, bs), (state_hbm, st), (wide_hbm, wide), (tall_hbm, tall), (accum_hbm, ac)]
         )
     ]
     for load in loads:
         load.start()
 
+    lane = lax.broadcasted_iota(jnp.int32, (1, 128), 1)
+    first = lane < CHUNK
+    sign = jnp.where(first, -1.0, 1.0)
+
+    def swap_halves(value):
+        return pltpu.roll(value, CHUNK, 1)
+
     loads[0].wait()
-    unit = (
-        lax.broadcasted_iota(jnp.int32, (rows_y, rows_y), 0)
-        == lax.broadcasted_iota(jnp.int32, (rows_y, rows_y), 1)
+    place = (
+        lax.broadcasted_iota(jnp.int32, (16, 128), 1) % CHUNK
+        == lax.broadcasted_iota(jnp.int32, (16, 128), 0) + row * 16
     ).astype(F32)
-    source_lane = lax.broadcasted_iota(jnp.int32, (96, 384), 0)
-    place = (
-        lax.broadcasted_iota(jnp.int32, (96, 384), 1)
-        == source_lane // 16 * CHUNK + source_lane % 16 + row * 16
-    ).astype(F32)
-    for level in range(LEVELS):
-        turned = exact(unit, bs[:, level].reshape(96, rows_y), ((1,), (1,)))
-        b0[level] = exact(turned, place, ((1,), (0,)))
+    placed = lax.dot_general(
+        bs[...].reshape(6 * LEVELS * rows_y, 16), place, (((1,), (0,)), ((), ())),
+        precision=lax.Precision.HIGHEST, preferred_element_type=F32,
+    ).reshape(6, LEVELS, rows_y, 128)
+    for q in range(3):
+        for level in range(LEVELS):
+            b0[level, :, 128 * q : 128 * (q + 1)] = jnp.where(
+                first, placed[2 * q, level], placed[2 * q + 1, level]
+            )
 
     kappa_y, signed_y = wave_numbers((ROWS, 1), 0, pen * ROWS)
     kappa_x, signed_x = wave_numbers((1, GRID), 1, 0)
@@ -134,16 +133,13 @@
         wzr, wzi = kappa_x * zr - kappa_y * zi, kappa_x * zi + kappa_y * zr
         wtr, wti = kappa_x * tr - kappa_y * ti, kappa_x * ti + kappa_y * tr
         packed = jnp.concatenate(
-            [
-                jnp.concatenate([wzr * inverse, wzi * inverse], axis=1),
-                jnp.concatenate([-wzi, wzr], axis=1),
-                jnp.concatenate([-wti, wtr], axis=1),
-            ],
-            axis=0,
-        )
-        mixed = product(split(packed), (xt[0], xt[1]))
+            [wzr * inverse, -wzi, -wti, wzi * inverse, wzr, wtr], axis=0
+        )
+        mixed = product(split(packed), (wide[0], wide[1]))
         for c in range(4):
-            xs[level, c] = mixed[:, 128 * c : 128 * (c + 1)].reshape(3, ROWS, 128)
+            even = mixed[: 3 * ROWS, 128 * c : 128 * (c + 1)]
+            odd = mixed[3 * ROWS :, 128 * c : 128 * (c + 1)]
+            xs[level, c] = (even + sign * swap_halves(odd)).reshape(3, ROWS, 128)
 
     def forward(level, c):
         target = c * 4 + level
@@ -221,7 +217,7 @@
     for k in range(1, groups):
         gather(k).start()
 
-    loads[3].wait()
+    loads[4].wait()
     for level in range(LEVELS):
         up, down = min(level + 1, LEVELS - 1), max(level - 1, 0)
         zr, zi = st[0, level, :, :GRID], st[0, level, :, GRID:]
@@ -254,7 +250,6 @@
     )
     swap.start()
 
-    loads[4].wait()
     own.wait()
 
     def forward_from(k):
@@ -271,21 +266,19 @@
     for k in range(1, PEN):
         forward_from(k).wait_recv()
 
-    table = (yt[0], yt[1])
+    loads[3].wait()
+    table = (tall[0], tall[1])
     spectral = jnp.concatenate([g[:, f].reshape(GRID, 128) for f in range(3)], axis=1)
     turned = product(table, split(spectral))
-    lane = lax.broadcasted_iota(jnp.int32, (1, 128), 1)
-    first = lane < CHUNK
-    sign = jnp.where(first, -1.0, 1.0)
-
-    def swap_halves(value):
-        return pltpu.roll(value, CHUNK, 1)
+    def blocks(value, part):
+        return jnp.concatenate(
+            [value[128 * c + CHUNK * part : 128 * c + CHUNK * (part + 1)] for c in range(4)], axis=0
+        )
 
     physical = []
     for f in range(3):
-        even = turned[:GRID, 128 * f : 128 * (f + 1)]
-        odd = turned[GRID:, 128 * f : 128 * (f + 1)]
-        physical.append(even + sign * swap_halves(odd))
+        one = turned[:, 128 * f : 128 * (f + 1)]
+        physical.append(blocks(one, 0) + sign * swap_halves(blocks(one, 1)))
 
     pltpu.make_async_remote_copy(
         src_ref=bb.at[:, 1 - core],
@@ -303,7 +296,7 @@
         first, advect_vort + swap_halves(advect_vort), advect_buoy + swap_halves(advect_buoy)
     )
     spread_y = product(table, split(advect))
-    real, imag = spread_y[:GRID], -spread_y[GRID:]
+    real, imag = blocks(spread_y, 0), -blocks(spread_y, 1)
     ys[:, 0] = jnp.where(first, real, swap_halves(imag)).reshape(PEN, ROWS, 128)
     ys[:, 1] = jnp.where(first, swap_halves(real), imag).reshape(PEN, ROWS, 128)
 
@@ -332,25 +325,24 @@
             if k != 0 or m != 0:
                 backward((column + m) % 4 * 4 + (row + k) % 4).start()
     h[pen] = ys[pen]
-    loads[5].wait()
     for k in range(1, PEN):
         backward_from((pen + k) % PEN).wait_recv()
 
-    gathered_x = jnp.concatenate([h[4 * c : 4 * c + 4].reshape(128, 128) for c in range(4)], axis=1)
-    spectra = product(split(gathered_x), (xf[0], xf[1]))
+    chunks = [h[4 * c : 4 * c + 4].reshape(128, 128) for c in range(4)]
+    gathered_x = jnp.concatenate(
+        [jnp.concatenate(chunks, axis=1),
+         jnp.concatenate([-sign * swap_halves(chunk) for chunk in chunks], axis=1)], axis=0
+    )
+    spectra = product(split(gathered_x), table)
     step = weight_factor * time_step
     for level in range(LEVELS):
         for field in range(2):
             start = (level * 2 + field) * ROWS
-            value = lin[field, level] - spectra[start : start + ROWS]
-            lin[field, level] = value
-            st[field, level] = st[field, level] + step * value
-    outs = [
-        pltpu.make_async_copy(lin, accum_next, out_sem.at[0]),
-        pltpu.make_async_copy(st, state_next, out_sem.at[1]),
-    ]
-    for out in outs:
-        out.start()
+            for part in range(2):
+                at = slice(GRID * part, GRID * (part + 1))
+                value = lin[field, level, :, at] - spectra[128 * part + start : 128 * part + start + ROWS]
+                accum_next[field, level, :, at] = value
+                state_next[field, level, :, at] = st[field, level, :, at] + step * value
 
     for k in (1, 2, 3):
         spread_from(k).wait_send()
@@ -360,28 +352,25 @@
     for k in range(1, PEN):
         forward_from(k).wait_send()
         backward_from((pen + k) % PEN).wait_send()
-    for out in outs:
-        out.wait()
 
 
 def on_device(groups, state, accum, base_flow):
     rows_y = GRID // (2 * groups)
-    x_inverse, y_table, x_forward = tables()
+    wide, tall = tables()
     fields = (2, LEVELS, ROWS, 2 * GRID)
     result = jax.ShapeDtypeStruct(fields, F32)
     dma = pltpu.SemaphoreType.DMA
     outputs = pl.pallas_call(
         functools.partial(kernel, groups),
         out_shape=(result, result),
-        in_specs=[pl.BlockSpec(memory_space=pl.ANY)] * 6,
-        out_specs=(pl.BlockSpec(memory_space=pl.ANY),) * 2,
+        in_specs=[pl.BlockSpec(memory_space=pltpu.HBM)] * 5,
+        out_specs=(pl.BlockSpec(memory_space=pltpu.VMEM),) * 2,
         scratch_shapes=[
             pltpu.VMEM(fields, F32),
             pltpu.VMEM(fields, F32),
-            pltpu.VMEM((6, LEVELS, 16, rows_y), F32),
-            pltpu.VMEM((2, 2 * GRID, 2 * GRID), BF16),
+            pltpu.VMEM((6, LEVELS, rows_y, 16), F32),
+            pltpu.VMEM((2, GRID, 2 * GRID), BF16),
             pltpu.VMEM((2, 2 * GRID, GRID), BF16),
-            pltpu.VMEM((2, 2 * GRID, 2 * GRID), BF16),
             pltpu.VMEM((LEVELS, 4, 3, ROWS, 128), F32),
             pltpu.VMEM((PEN, 3, ROWS, 128), F32),
             pltpu.VMEM((LEVELS, rows_y, 384), F32),
@@ -390,8 +379,7 @@
             pltpu.VMEM((PEN, 2, ROWS, 128), F32),
             pltpu.VMEM((PEN, 2, ROWS, 128), F32),
             pltpu.VMEM(fields, F32),
-            dma((6,)),
-            dma((2,)),
+            dma((5,)),
             dma((PEN,)),
             dma((PEN,)),
             dma((PEN,)),
@@ -408,9 +396,9 @@
             collective_id=0, has_side_effects=True, vmem_limit_bytes=40 * 1024 * 1024
         ),
         name="step",
-    )(
-        state.reshape(fields), accum.reshape(fields), base_flow,
-        jnp.asarray(x_inverse), jnp.asarray(y_table), jnp.asarray(x_forward),
+    )(*[pltpu.with_memory_space_constraint(x, pltpu.HBM) for x in (
+        state.reshape(fields), accum.reshape(fields), base_flow.transpose(0, 1, 3, 2),
+        jnp.asarray(wide), jnp.asarray(tall))]
     )
     return tuple(out.reshape(state.shape) for out in outputs)
 

time: 49.8 us -> 43.8 us (0.88)
  local copies, waits for them, and re-layouts: 6.89 us -> 1.41 us
    unnamed x13 -> x2, local copies, waits for them, and re-layouts: 6.89 us -> 1.41 us
where the time goes in v2:
time: 43.8 us; the launch traced here: 43.6 us
  Pallas kernels  41.6 us (95%)
  local copies, waits for them, and re-layouts  1.41 us (3%)
  between operations  0.64 us (1%)
    pallas_call x1, Pallas kernels, on_device(): pl.pallas_call(functools.partial(kernel, groups), out_shape=(result, resu...  41.6 us
    unnamed x2, local copies, waits for them, and re-layouts  1.41 us

profile of v2, /device:TPU:1, one launch (start us, length us, event | category | flops | bytes accessed | tf_op | source)
XLA Modules:
  0.0 43.6 jit_solution(15251437809789287358)
XLA Ops:
  0.6 41.6 %step.1 = (f32[2,4,16,512]{3,2,1,0:T(8,128)S(1)}, f32[2,4,16,512]{3,2,1,0:T(8,128)S(1)}) custom-call(f32[2,4,16,512]{3,2,1,0:T(8,128)} %bitcast.11, f32[2,4,16,512]{3,2,1,0:T(8,128)} %bitcast.12, f32[6,4,8,16]{3,2,1,0:T(8,128)} %bitcast.13, bf16[2,256,512]{2,1,0:T(8,128)(2,1)} %constant.4.clone.wide_hbm, bf16[2,512,256]{2,1,0:T(8,128)(2,1)} %constant.5.clone.tall_hbm), custom_call_target="tpu_custom_call" | custom-call | tf_op jit(solution)/shard_map/step/pallas_call | solution.py:363
  42.2 0.7 %copy.11 = f32[2,1,4,16,512]{4,3,2,1,0:T(8,128)} copy(f32[2,1,4,16,512]{4,3,2,1,0:T(8,128)S(1)} %bitcast.10) | data formatting | bytes 524288
  42.9 0.7 %copy.12 = f32[2,1,4,16,512]{4,3,2,1,0:T(8,128)} copy(f32[2,1,4,16,512]{4,3,2,1,0:T(8,128)S(1)} %bitcast.9) | data formatting | bytes 524288

commit v3 on v2

v3 whole, which is shorter than its diff:
```python
import functools
import math

import jax
import jax.numpy as jnp
import numpy as np
from jax import lax
from jax.experimental import pallas as pl
from jax.experimental.pallas import tpu as pltpu
from jax.sharding import PartitionSpec as P

viscosity = 0.05
vertical_mixing = 0.5
buoyancy_gain = 0.5
stratification = 0.5
memory_factor = -5.0 / 9.0
weight_factor = 15.0 / 16.0
time_step = 0.4

GRID = 256
LEVELS = 4
ROWS = 16
PEN = 16
CHUNK = 16
MESH = pl.DeviceIdType.MESH
F32 = jnp.float32
BF16 = jnp.bfloat16


def halves(table):
    high = table.astype(np.float32).astype(jnp.bfloat16)
    low = (table - high.astype(np.float64)).astype(np.float32).astype(jnp.bfloat16)
    return np.stack([high, low])


def tables():
    position = np.arange(GRID)
    angle = 2.0 * np.pi / GRID * (position[:, None] * position[None, :] % GRID)
    table = np.stack([np.cos(angle), np.sin(angle)], 1).reshape(GRID, 2, GRID // CHUNK, CHUNK)
    table = table.transpose(0, 2, 1, 3).reshape(GRID, 2 * GRID) / 16.0
    return halves(table), halves(table.T.copy())


def split(value):
    high = value.astype(BF16)
    return high, (value - high.astype(F32)).astype(BF16)


def dot(a, b):
    return jnp.dot(a, b, preferred_element_type=F32)


def product(a, b):
    return dot(a[0], b[0]) + (dot(a[1], b[0]) + dot(a[0], b[1]))


def wave_numbers(shape, dim, offset):
    position = lax.broadcasted_iota(jnp.int32, shape, dim) + offset
    signed = jnp.where(position <= GRID // 2, position, position - GRID)
    derivative = jnp.where(position == GRID // 2, 0, signed)
    return (2.0 * math.pi / GRID) * derivative.astype(F32), signed


def kernel(
    groups,
    state_hbm, accum_hbm, base_hbm, wide_hbm, tall_hbm,
    state_next, accum_next,
    st, ac, bs, wide, tall, pk_high, pk_low, xs, g, bb, ys, h, lin,
    load_sem, fs, fr, rs, rr, cs, cr, hs, hr, own_sem, here,
):
    ens = lax.axis_index("ens")
    pen = lax.axis_index("pen")
    pair, core = ens // 2, ens % 2
    column, row = pen // 4, pen % 4
    other = ens + 1 - 2 * core
    rows_y = GRID // (2 * groups)

    barrier = pltpu.get_barrier_semaphore()
    for k in range(1, PEN):
        pl.semaphore_signal(barrier, inc=1, device_id=(ens, (pen + k) % PEN), device_id_type=MESH)
    pl.semaphore_signal(barrier, inc=1, device_id=(other, pen), device_id_type=MESH)
    for k in range(1, groups):

        @pl.when(pair + k < groups)
        def _():
            pl.semaphore_signal(
                barrier, inc=1, device_id=((pair + k) * 2 + core, pen), device_id_type=MESH
            )

    loads = [
        pltpu.make_async_copy(source, target, load_sem.at[i])
        for i, (source, target) in enumerate(
            [(base_hbm, bs), (state_hbm, st), (wide_hbm, wide), (tall_hbm, tall), (accum_hbm, ac)]
        )
    ]
    for load in loads:
        load.start()

    lane = lax.broadcasted_iota(jnp.int32, (1, 128), 1)
    first = lane // CHUNK % 2 == 0
    sign = jnp.where(first, -1.0, 1.0)

    def swap_parts(value):
        return jnp.where(
            first, pltpu.roll(value, 128 - CHUNK, 1), pltpu.roll(value, CHUNK, 1)
        )

    def turn(values):
        results = []
        for j in range(4):
            result = None
            for l in range(4):
                moved = values[l] if l == j else pltpu.roll(values[l], 32 * (l - j) % 128, 1)
                result = moved if result is None else jnp.where(lane // 32 == l, moved, result)
            results.append(result)
        return results

    loads[0].wait()
    place = (
        lax.broadcasted_iota(jnp.int32, (CHUNK, 128), 1) % CHUNK
        == lax.broadcasted_iota(jnp.int32, (CHUNK, 128), 0)
    ).astype(F32)
    placed = lax.dot_general(
        bs[...].reshape(6 * LEVELS * rows_y, CHUNK), place, (((1,), (0,)), ((), ())),
        precision=lax.Precision.HIGHEST, preferred_element_type=F32,
    ).reshape(6, LEVELS, rows_y, 128)
    for q in range(3):
        result = placed[2 * q, 0]
        for group in range(1, 8):
            result = jnp.where(
                lane // CHUNK == group, placed[2 * q + group % 2, group // 2], result
            )
        bb[pair, core, :, 128 * q : 128 * (q + 1)] = result

    def gather(target):
        return pltpu.make_async_remote_copy(
            src_ref=bb.at[pair, core],
            dst_ref=bb.at[pair, core],
            send_sem=hs.at[target],
            recv_sem=hr.at[pair],
            device_id=(target * 2 + core, pen),
            device_id_type=MESH,
        )

    def gathered(source):
        return pltpu.make_async_remote_copy(
            src_ref=bb.at[source, core],
            dst_ref=bb.at[source, core],
            send_sem=hs.at[source],
            recv_sem=hr.at[source],
            device_id=(source * 2 + core, pen),
            device_id_type=MESH,
        )

    pl.semaphore_wait(barrier, PEN + pair)
    for k in range(1, groups):

        @pl.when(pair - k >= 0)
        def _():
            pl.semaphore_signal(
                here.at[pair], inc=1, device_id=((pair - k) * 2 + core, pen), device_id_type=MESH
            )
            gather(pair - k).start()

    kappa_y, signed_y = wave_numbers((ROWS, 1), 0, pen * ROWS)
    kappa_x, signed_x = wave_numbers((1, GRID), 1, 0)
    wave_square = signed_y * signed_y + signed_x * signed_x
    factor = (2.0 * math.pi / GRID) ** 2
    square = factor * wave_square.astype(F32)
    inverse = jnp.where(
        wave_square > 0, 1.0 / (factor * jnp.maximum(wave_square, 1).astype(F32)), 0.0
    )

    loads[1].wait()
    loads[2].wait()

    packed = []
    for level in range(LEVELS):
        zr, zi = st[0, level, :, :GRID], st[0, level, :, GRID:]
        tr, ti = st[1, level, :, :GRID], st[1, level, :, GRID:]
        wzr, wzi = kappa_x * zr - kappa_y * zi, kappa_x * zi + kappa_y * zr
        wtr, wti = kappa_x * tr - kappa_y * ti, kappa_x * ti + kappa_y * tr
        packed += [wzr * inverse, -wzi, -wti, wzi * inverse, wzr, wtr]
    pk_high[...], pk_low[...] = split(jnp.concatenate(packed, axis=0))

    def forward(target):
        return pltpu.make_async_remote_copy(
            src_ref=xs.at[target],
            dst_ref=g.at[pen],
            send_sem=fs.at[target],
            recv_sem=fr.at[pen],
            device_id=(ens, target),
            device_id_type=MESH,
        )

    for m in (2, 1, 3, 0):
        to = (column + m) % 4
        at = pl.ds(pl.multiple_of(to * 128, 128), 128)
        mixed = product((pk_high[...], pk_low[...]), (wide[0, :, at], wide[1, :, at]))
        mixed = mixed.reshape(LEVELS, 2, 3 * ROWS, 128)
        parts = turn([mixed[l, 0] + sign * swap_parts(mixed[l, 1]) for l in range(LEVELS)])
        for j in range(4):
            xs[to * 4 + j] = parts[j].reshape(3, ROWS, 128)
        for k in (2, 1, 3, 0):
            if k != 0 or m != 0:
                forward(to * 4 + (row + k) % 4).start()
    own = pltpu.make_async_copy(xs.at[pen], g.at[pen], own_sem.at[0])
    own.start()
    for k in range(1, groups):

        @pl.when(pair + k < groups)
        def _():
            pl.semaphore_wait(here.at[pair + k], 1)
            gather(pair + k).start()

    loads[4].wait()
    for level in range(LEVELS):
        up, down = min(level + 1, LEVELS - 1), max(level - 1, 0)
        zr, zi = st[0, level, :, :GRID], st[0, level, :, GRID:]
        tr, ti = st[1, level, :, :GRID], st[1, level, :, GRID:]
        across = stratification * kappa_x * inverse
        linear = (
            jnp.concatenate([-buoyancy_gain * kappa_x * ti, buoyancy_gain * kappa_x * tr], axis=1),
            jnp.concatenate([-across * zi, across * zr], axis=1),
        )
        damping = viscosity * jnp.concatenate([square, square], axis=1)
        for field in range(2):
            value = st[field, level]
            mixing = st[field, up] + st[field, down] - 2.0 * value
            lin[field, level] = (
                memory_factor * ac[field, level]
                + linear[field]
                - damping * value
                + vertical_mixing * mixing
            )

    half = groups // 2

    def swap(part, side):
        return pltpu.make_async_remote_copy(
            src_ref=bb.at[half * part : half * (part + 1), side],
            dst_ref=bb.at[half * part : half * (part + 1), side],
            send_sem=cs.at[part],
            recv_sem=cr.at[part],
            device_id=(other, pen),
            device_id_type=MESH,
        )

    for part in range(2):
        for source in range(half * part, half * (part + 1)):

            @pl.when(pair != source)
            def _():
                gathered(source).wait_recv()

        swap(part, core).start()

    own.wait()

    def forward_from(k):
        source = (pen + k) % PEN
        return pltpu.make_async_remote_copy(
            src_ref=xs.at[source],
            dst_ref=g.at[source],
            send_sem=fs.at[source],
            recv_sem=fr.at[source],
            device_id=(ens, source),
            device_id_type=MESH,
        )

    for k in range(1, PEN):
        forward_from(k).wait_recv()

    loads[3].wait()
    table = (tall[0], tall[1])
    spectral = jnp.concatenate([g[:, f].reshape(GRID, 128) for f in range(3)], axis=1)
    turned = product(table, split(spectral))
    def blocks(value, part):
        rows = value.reshape(value.shape[0] // 32, 2, CHUNK, 128)[:, part]
        return rows.reshape(value.shape[0] // 2, 128)

    physical = []
    for f in range(3):
        one = turned[:, 128 * f : 128 * (f + 1)]
        physical.append(blocks(one, 0) + sign * swap_parts(blocks(one, 1)))

    for part in range(2):
        swap(part, 1 - core).wait_recv()
    base = bb[...].reshape(GRID, 384)
    flow, vort_slope, buoy_slope = base[:, :128], base[:, 128:256], base[:, 256:]
    advect_vort = flow * physical[1] + vort_slope * physical[0]
    advect_buoy = flow * physical[2] + buoy_slope * physical[0]
    advect = jnp.where(
        first, advect_vort + swap_parts(advect_vort), advect_buoy + swap_parts(advect_buoy)
    )
    adverse = split(advect)

    def backward(target):
        return pltpu.make_async_remote_copy(
            src_ref=ys.at[target],
            dst_ref=h.at[pen],
            send_sem=rs.at[target],
            recv_sem=rr.at[pen],
            device_id=(ens, target),
            device_id_type=MESH,
        )

    def backward_from(source):
        return pltpu.make_async_remote_copy(
            src_ref=ys.at[source],
            dst_ref=h.at[source],
            send_sem=rs.at[source],
            recv_sem=rr.at[source],
            device_id=(ens, source),
            device_id_type=MESH,
        )

    for m in (2, 1, 3, 0):
        to = (column + m) % 4
        rows = pl.ds(pl.multiple_of(to * 128, 128), 128)
        spread_y = product((tall[0, rows], tall[1, rows]), adverse)
        real, imag = blocks(spread_y, 0), -blocks(spread_y, 1)
        four = pl.ds(to * 4, 4)
        ys[four, 0] = jnp.where(first, real, swap_parts(imag)).reshape(4, ROWS, 128)
        ys[four, 1] = jnp.where(first, swap_parts(real), imag).reshape(4, ROWS, 128)
        for k in (2, 1, 3, 0):
            if k != 0 or m != 0:
                backward(to * 4 + (row + k) % 4).start()
    h[pen] = ys[pen]

    step = weight_factor * time_step
    for k in range(1, PEN):
        backward_from((pen + k) % PEN).wait_recv()
    turned_x = [turn([h[4 * q + j].reshape(2 * ROWS, 128) for j in range(4)]) for q in range(4)]
    for level in range(LEVELS):
        chunks = [turned_x[q][level] for q in range(4)]
        gathered_x = jnp.concatenate(
            [jnp.concatenate(chunks, axis=1),
             jnp.concatenate([-sign * swap_parts(chunk) for chunk in chunks], axis=1)], axis=0
        )
        spectra = product(split(gathered_x), table)
        for field in range(2):
            for part in range(2):
                at = slice(GRID * part, GRID * (part + 1))
                start = (2 * part + field) * ROWS
                value = lin[field, level, :, at] - spectra[start : start + ROWS]
                accum_next[field, level, :, at] = value
                state_next[field, level, :, at] = st[field, level, :, at] + step * value

    for k in range(1, groups):
        gather((pair + k) % groups).wait_send()
    for part in range(2):
        swap(part, core).wait_send()
    for k in range(1, PEN):
        forward_from(k).wait_send()
        backward_from((pen + k) % PEN).wait_send()


def on_device(groups, state, accum, base_flow):
    rows_y = GRID // (2 * groups)
    wide, tall = tables()
    fields = (2, LEVELS, ROWS, 2 * GRID)
    result = jax.ShapeDtypeStruct(fields, F32)
    dma = pltpu.SemaphoreType.DMA
    outputs = pl.pallas_call(
        functools.partial(kernel, groups),
        out_shape=(result, result),
        in_specs=[pl.BlockSpec(memory_space=pltpu.HBM)] * 5,
        out_specs=(pl.BlockSpec(memory_space=pltpu.VMEM),) * 2,
        scratch_shapes=[
            pltpu.VMEM(fields, F32),
            pltpu.VMEM(fields, F32),
            pltpu.VMEM((6, LEVELS, rows_y, 16), F32),
            pltpu.VMEM((2, GRID, 2 * GRID), BF16),
            pltpu.VMEM((2, 2 * GRID, GRID), BF16),
            pltpu.VMEM((6 * LEVELS * ROWS, GRID), BF16),
            pltpu.VMEM((6 * LEVELS * ROWS, GRID), BF16),
            pltpu.VMEM((PEN, 3, ROWS, 128), F32),
            pltpu.VMEM((PEN, 3, ROWS, 128), F32),
            pltpu.VMEM((groups, 2, rows_y, 384), F32),
            pltpu.VMEM((PEN, 2, ROWS, 128), F32),
            pltpu.VMEM((PEN, 2, ROWS, 128), F32),
            pltpu.VMEM(fields, F32),
            dma((5,)),
            dma((PEN,)),
            dma((PEN,)),
            dma((PEN,)),
            dma((PEN,)),
            dma((2,)),
            dma((2,)),
            dma((groups,)),
            dma((groups,)),
            dma((1,)),
            pltpu.SemaphoreType.REGULAR((groups,)),
        ],
        compiler_params=pltpu.CompilerParams(
            collective_id=0, has_side_effects=True, vmem_limit_bytes=40 * 1024 * 1024
        ),
        name="step",
    )(*[pltpu.with_memory_space_constraint(x, pltpu.HBM) for x in (
        state.reshape(fields), accum.reshape(fields), base_flow.transpose(0, 1, 3, 2),
        jnp.asarray(wide), jnp.asarray(tall))]
    )
    return tuple(out.reshape(state.shape) for out in outputs)


def solution(mesh):
    spectral = P(None, "ens", None, "pen", None)
    return jax.shard_map(
        functools.partial(on_device, mesh.shape["ens"] // 2),
        mesh=mesh,
        in_specs=(spectral, spectral, P(None, None, "pen", "ens")),
        out_specs=(spectral, spectral),
        check_vma=False,
    )
```

time: 43.8 us -> 38.2 us (0.87)
  Pallas kernels: 41.6 us -> 36 us
    pallas_call x1, Pallas kernels: 41.6 us -> 36 us  [on_device(): pl.pallas_call(functools.partial(kernel, groups), out_shape=(result, resu...]
where the time goes in v3:
time: 38.2 us; the launch traced here: 38.1 us
  Pallas kernels  36 us (94%)
  local copies, waits for them, and re-layouts  1.41 us (4%)
  between operations  0.64 us (2%)
    pallas_call x1, Pallas kernels, on_device(): pl.pallas_call(functools.partial(kernel, groups), out_shape=(result, resu...  36 us
    unnamed x2, local copies, waits for them, and re-layouts  1.41 us

profile of v3, /device:TPU:1, one launch (start us, length us, event | category | flops | bytes accessed | tf_op | source)
XLA Modules:
  0.0 38.1 jit_solution(3609157827485477769)
XLA Ops:
  0.6 36.0 %step.1 = (f32[2,4,16,512]{3,2,1,0:T(8,128)S(1)}, f32[2,4,16,512]{3,2,1,0:T(8,128)S(1)}) custom-call(f32[2,4,16,512]{3,2,1,0:T(8,128)} %bitcast.11, f32[2,4,16,512]{3,2,1,0:T(8,128)} %bitcast.12, f32[6,4,8,16]{3,2,1,0:T(8,128)} %bitcast.13, bf16[2,256,512]{2,1,0:T(8,128)(2,1)} %constant.4.clone.wide_hbm, bf16[2,512,256]{2,1,0:T(8,128)(2,1)} %constant.5.clone.tall_hbm), custom_call_target="tpu_custom_call" | custom-call | tf_op jit(solution)/shard_map/step/pallas_call | solution.py:365
  36.7 0.7 %copy.11 = f32[2,1,4,16,512]{4,3,2,1,0:T(8,128)} copy(f32[2,1,4,16,512]{4,3,2,1,0:T(8,128)S(1)} %bitcast.10) | data formatting | bytes 524288
  37.4 0.7 %copy.12 = f32[2,1,4,16,512]{4,3,2,1,0:T(8,128)} copy(f32[2,1,4,16,512]{4,3,2,1,0:T(8,128)S(1)} %bitcast.9) | data formatting | bytes 524288

commit v4 on v3

--- a/solution.py
+++ b/solution.py
@@ -66,7 +66,7 @@
     state_hbm, accum_hbm, base_hbm, wide_hbm, tall_hbm,
     state_next, accum_next,
     st, ac, bs, wide, tall, pk_high, pk_low, xs, g, bb, ys, h, lin,
-    load_sem, fs, fr, rs, rr, cs, cr, hs, hr, own_sem, here,
+    load_sem, fs, fr, rs, rr, cs, cr, hs, hr, here,
 ):
     ens = lax.axis_index("ens")
     pen = lax.axis_index("pen")
@@ -114,6 +114,20 @@
                 result = moved if result is None else jnp.where(lane // 32 == l, moved, result)
             results.append(result)
         return results
+
+    half = groups // 2
+    quarter = groups // 4
+    pl.semaphore_wait(barrier, PEN + pair)
+    for k in range(1, groups):
+
+        @pl.when(pair - k >= 0)
+        def _():
+            pl.semaphore_signal(
+                here.at[pair // half],
+                inc=1,
+                device_id=((pair - k) * 2 + core, pen),
+                device_id_type=MESH,
+            )
 
     loads[0].wait()
     place = (
@@ -136,31 +150,27 @@
         return pltpu.make_async_remote_copy(
             src_ref=bb.at[pair, core],
             dst_ref=bb.at[pair, core],
-            send_sem=hs.at[target],
-            recv_sem=hr.at[pair],
+            send_sem=hs.at[0],
+            recv_sem=hr.at[pair // quarter],
             device_id=(target * 2 + core, pen),
             device_id_type=MESH,
         )
 
-    def gathered(source):
-        return pltpu.make_async_remote_copy(
-            src_ref=bb.at[source, core],
-            dst_ref=bb.at[source, core],
-            send_sem=hs.at[source],
-            recv_sem=hr.at[source],
-            device_id=(source * 2 + core, pen),
-            device_id_type=MESH,
-        )
-
-    pl.semaphore_wait(barrier, PEN + pair)
-    for k in range(1, groups):
-
-        @pl.when(pair - k >= 0)
-        def _():
-            pl.semaphore_signal(
-                here.at[pair], inc=1, device_id=((pair - k) * 2 + core, pen), device_id_type=MESH
-            )
-            gather(pair - k).start()
+    def pieces(count, sem):
+        return pltpu.make_async_remote_copy(
+            src_ref=bb.at[:count, 0],
+            dst_ref=bb.at[:count, 0],
+            send_sem=hs.at[0],
+            recv_sem=sem,
+            device_id=(other, pen),
+            device_id_type=MESH,
+        )
+
+    for target in range(groups - 1):
+
+        @pl.when(target < pair)
+        def _():
+            gather(target).start()
 
     kappa_y, signed_y = wave_numbers((ROWS, 1), 0, pen * ROWS)
     kappa_x, signed_x = wave_numbers((1, GRID), 1, 0)
@@ -187,8 +197,8 @@
         return pltpu.make_async_remote_copy(
             src_ref=xs.at[target],
             dst_ref=g.at[pen],
-            send_sem=fs.at[target],
-            recv_sem=fr.at[pen],
+            send_sem=fs.at[0],
+            recv_sem=fr.at[0],
             device_id=(ens, target),
             device_id_type=MESH,
         )
@@ -204,14 +214,20 @@
         for k in (2, 1, 3, 0):
             if k != 0 or m != 0:
                 forward(to * 4 + (row + k) % 4).start()
-    own = pltpu.make_async_copy(xs.at[pen], g.at[pen], own_sem.at[0])
-    own.start()
-    for k in range(1, groups):
-
-        @pl.when(pair + k < groups)
-        def _():
-            pl.semaphore_wait(here.at[pair + k], 1)
-            gather(pair + k).start()
+    g[pen] = xs[pen]
+    for part in range(2):
+        waits = jnp.where(pair // half == part, half * (part + 1) - 1 - pair, half)
+        waits = jnp.where(pair // half > part, 0, waits)
+
+        @pl.when(waits > 0)
+        def _():
+            pl.semaphore_wait(here.at[part], waits)
+
+        for target in range(half * part, half * (part + 1)):
+
+            @pl.when(pair < target)
+            def _():
+                gather(target).start()
 
     loads[4].wait()
     for level in range(LEVELS):
@@ -234,42 +250,39 @@
                 + vertical_mixing * mixing
             )
 
-    half = groups // 2
-
     def swap(part, side):
         return pltpu.make_async_remote_copy(
-            src_ref=bb.at[half * part : half * (part + 1), side],
-            dst_ref=bb.at[half * part : half * (part + 1), side],
-            send_sem=cs.at[part],
-            recv_sem=cr.at[part],
+            src_ref=bb.at[quarter * part : quarter * (part + 1), side],
+            dst_ref=bb.at[quarter * part : quarter * (part + 1), side],
+            send_sem=cs.at[0],
+            recv_sem=cr.at[0],
             device_id=(other, pen),
             device_id_type=MESH,
         )
 
-    for part in range(2):
-        for source in range(half * part, half * (part + 1)):
-
-            @pl.when(pair != source)
-            def _():
-                gathered(source).wait_recv()
+    for part in range(4):
+
+        @pl.when(pair // quarter == part)
+        def _():
+            pieces(quarter - 1, hr.at[part]).wait_recv()
+
+        @pl.when(pair // quarter != part)
+        def _():
+            pieces(quarter, hr.at[part]).wait_recv()
 
         swap(part, core).start()
 
-    own.wait()
-
-    def forward_from(k):
-        source = (pen + k) % PEN
-        return pltpu.make_async_remote_copy(
-            src_ref=xs.at[source],
-            dst_ref=g.at[source],
-            send_sem=fs.at[source],
-            recv_sem=fr.at[source],
-            device_id=(ens, source),
-            device_id_type=MESH,
-        )
-
-    for k in range(1, PEN):
-        forward_from(k).wait_recv()
+    def others(sent, received, sems):
+        return pltpu.make_async_remote_copy(
+            src_ref=sent.at[: PEN - 1],
+            dst_ref=received.at[: PEN - 1],
+            send_sem=sems[0].at[0],
+            recv_sem=sems[1].at[0],
+            device_id=(other, pen),
+            device_id_type=MESH,
+        )
+
+    others(xs, g, (fs, fr)).wait_recv()
 
     loads[3].wait()
     table = (tall[0], tall[1])
@@ -284,8 +297,15 @@
         one = turned[:, 128 * f : 128 * (f + 1)]
         physical.append(blocks(one, 0) + sign * swap_parts(blocks(one, 1)))
 
-    for part in range(2):
-        swap(part, 1 - core).wait_recv()
+    whole_swap = pltpu.make_async_remote_copy(
+        src_ref=bb.at[:, 0],
+        dst_ref=bb.at[:, 0],
+        send_sem=cs.at[0],
+        recv_sem=cr.at[0],
+        device_id=(other, pen),
+        device_id_type=MESH,
+    )
+    whole_swap.wait_recv()
     base = bb[...].reshape(GRID, 384)
     flow, vort_slope, buoy_slope = base[:, :128], base[:, 128:256], base[:, 256:]
     advect_vort = flow * physical[1] + vort_slope * physical[0]
@@ -299,19 +319,9 @@
         return pltpu.make_async_remote_copy(
             src_ref=ys.at[target],
             dst_ref=h.at[pen],
-            send_sem=rs.at[target],
-            recv_sem=rr.at[pen],
+            send_sem=rs.at[0],
+            recv_sem=rr.at[0],
             device_id=(ens, target),
-            device_id_type=MESH,
-        )
-
-    def backward_from(source):
-        return pltpu.make_async_remote_copy(
-            src_ref=ys.at[source],
-            dst_ref=h.at[source],
-            send_sem=rs.at[source],
-            recv_sem=rr.at[source],
-            device_id=(ens, source),
             device_id_type=MESH,
         )
 
@@ -329,8 +339,7 @@
     h[pen] = ys[pen]
 
     step = weight_factor * time_step
-    for k in range(1, PEN):
-        backward_from((pen + k) % PEN).wait_recv()
+    others(ys, h, (rs, rr)).wait_recv()
     turned_x = [turn([h[4 * q + j].reshape(2 * ROWS, 128) for j in range(4)]) for q in range(4)]
     for level in range(LEVELS):
         chunks = [turned_x[q][level] for q in range(4)]
@@ -347,13 +356,10 @@
                 accum_next[field, level, :, at] = value
                 state_next[field, level, :, at] = st[field, level, :, at] + step * value
 
-    for k in range(1, groups):
-        gather((pair + k) % groups).wait_send()
-    for part in range(2):
-        swap(part, core).wait_send()
-    for k in range(1, PEN):
-        forward_from(k).wait_send()
-        backward_from((pen + k) % PEN).wait_send()
+    pieces(groups - 1, hr.at[0]).wait_send()
+    whole_swap.wait_send()
+    others(xs, g, (fs, fr)).wait_send()
+    others(ys, h, (rs, rr)).wait_send()
 
 
 def on_device(groups, state, accum, base_flow):
@@ -382,16 +388,15 @@
             pltpu.VMEM((PEN, 2, ROWS, 128), F32),
             pltpu.VMEM(fields, F32),
             dma((5,)),
-            dma((PEN,)),
-            dma((PEN,)),
-            dma((PEN,)),
-            dma((PEN,)),
-            dma((2,)),
-            dma((2,)),
-            dma((groups,)),
-            dma((groups,)),
-            dma((1,)),
-            pltpu.SemaphoreType.REGULAR((groups,)),
+            dma((1,)),
+            dma((1,)),
+            dma((1,)),
+            dma((1,)),
+            dma((1,)),
+            dma((1,)),
+            dma((1,)),
+            dma((4,)),
+            pltpu.SemaphoreType.REGULAR((2,)),
         ],
         compiler_params=pltpu.CompilerParams(
             collective_id=0, has_side_effects=True, vmem_limit_bytes=40 * 1024 * 1024

time: 38.2 us -> 35.4 us (0.927)
  Pallas kernels: 36 us -> 33.2 us
    pallas_call x1, Pallas kernels: 36 us -> 33.2 us  [on_device(): pl.pallas_call(functools.partial(kernel, groups), out_shape=(result, resu...]
where the time goes in v4:
time: 35.4 us; the launch traced here: 35.3 us
  Pallas kernels  33.2 us (94%)
  local copies, waits for them, and re-layouts  1.41 us (4%)
  between operations  0.64 us (2%)
    pallas_call x1, Pallas kernels, on_device(): pl.pallas_call(functools.partial(kernel, groups), out_shape=(result, resu...  33.2 us
    unnamed x2, local copies, waits for them, and re-layouts  1.41 us

profile of v4, /device:TPU:1, one launch (start us, length us, event | category | flops | bytes accessed | tf_op | source)
XLA Modules:
  0.0 35.3 jit_solution(17215269436973430468)
XLA Ops:
  0.6 33.2 %step.1 = (f32[2,4,16,512]{3,2,1,0:T(8,128)S(1)}, f32[2,4,16,512]{3,2,1,0:T(8,128)S(1)}) custom-call(f32[2,4,16,512]{3,2,1,0:T(8,128)} %bitcast.11, f32[2,4,16,512]{3,2,1,0:T(8,128)} %bitcast.12, f32[6,4,8,16]{3,2,1,0:T(8,128)} %bitcast.13, bf16[2,256,512]{2,1,0:T(8,128)(2,1)} %constant.4.clone.wide_hbm, bf16[2,512,256]{2,1,0:T(8,128)(2,1)} %constant.5.clone.tall_hbm), custom_call_target="tpu_custom_call" | custom-call | tf_op jit(solution)/shard_map/step/pallas_call | solution.py:371
  33.9 0.7 %copy.11 = f32[2,1,4,16,512]{4,3,2,1,0:T(8,128)} copy(f32[2,1,4,16,512]{4,3,2,1,0:T(8,128)S(1)} %bitcast.10) | data formatting | bytes 524288
  34.6 0.7 %copy.12 = f32[2,1,4,16,512]{4,3,2,1,0:T(8,128)} copy(f32[2,1,4,16,512]{4,3,2,1,0:T(8,128)S(1)} %bitcast.9) | data formatting | bytes 524288

commit v5 on v4

v5 whole, which is shorter than its diff:
```python
import functools
import math

import jax
import jax.numpy as jnp
import numpy as np
from jax import lax
from jax.experimental import pallas as pl
from jax.experimental.pallas import tpu as pltpu
from jax.sharding import PartitionSpec as P

viscosity = 0.05
vertical_mixing = 0.5
buoyancy_gain = 0.5
stratification = 0.5
memory_factor = -5.0 / 9.0
weight_factor = 15.0 / 16.0
time_step = 0.4

GRID = 256
LEVELS = 4
ROWS = 16
PEN = 16
CHUNK = 16
MESH = pl.DeviceIdType.MESH
F32 = jnp.float32
BF16 = jnp.bfloat16


def halves(table):
    high = table.astype(np.float32).astype(jnp.bfloat16)
    low = (table - high.astype(np.float64)).astype(np.float32).astype(jnp.bfloat16)
    return np.stack([high, low])


def tables():
    position = np.arange(GRID)
    angle = 2.0 * np.pi / GRID * (position[:, None] * position[None, :] % GRID)
    table = np.stack([np.cos(angle), np.sin(angle)], 1).reshape(GRID, 2, GRID // CHUNK, CHUNK)
    table = table.transpose(0, 2, 1, 3).reshape(GRID, 2 * GRID) / 16.0
    return halves(table), halves(table.T.copy())


def split(value):
    high = value.astype(BF16)
    return high, (value - high.astype(F32)).astype(BF16)


def dot(a, b):
    return jnp.dot(a, b, preferred_element_type=F32)


def product(a, b):
    return dot(a[0], b[0]) + (dot(a[1], b[0]) + dot(a[0], b[1]))


def wave_numbers(shape, dim, offset):
    position = lax.broadcasted_iota(jnp.int32, shape, dim) + offset
    signed = jnp.where(position <= GRID // 2, position, position - GRID)
    derivative = jnp.where(position == GRID // 2, 0, signed)
    return (2.0 * math.pi / GRID) * derivative.astype(F32), signed


def kernel(
    groups,
    state_hbm, accum_hbm, base_hbm, wide_hbm, tall_hbm,
    lin, advected,
    st, ac, bs, wide, tall, pk_high, pk_low, xs, g, bb, ys, h,
    load_sem, fs, fr, rs, rr, cs, cr, hs, hr, here,
):
    ens = lax.axis_index("ens")
    pen = lax.axis_index("pen")
    pair, core = ens // 2, ens % 2
    column, row = pen // 4, pen % 4
    other = ens + 1 - 2 * core
    rows_y = GRID // (2 * groups)

    loads = [
        pltpu.make_async_copy(source, target, load_sem.at[i])
        for i, (source, target) in enumerate(
            [(base_hbm, bs), (state_hbm, st), (wide_hbm, wide), (tall_hbm, tall), (accum_hbm, ac)]
        )
    ]
    for load in loads:
        load.start()

    barrier = pltpu.get_barrier_semaphore()
    for k in range(1, PEN):
        pl.semaphore_signal(barrier, inc=1, device_id=(ens, (pen + k) % PEN), device_id_type=MESH)
    pl.semaphore_signal(barrier, inc=1, device_id=(other, pen), device_id_type=MESH)
    for k in range(1, groups):

        @pl.when(pair + k < groups)
        def _():
            pl.semaphore_signal(
                barrier, inc=1, device_id=((pair + k) * 2 + core, pen), device_id_type=MESH
            )

    lane = lax.broadcasted_iota(jnp.int32, (1, 128), 1)
    first = lane // CHUNK % 2 == 0
    sign = jnp.where(first, -1.0, 1.0)

    def swap_parts(value):
        return jnp.where(
            first, pltpu.roll(value, 128 - CHUNK, 1), pltpu.roll(value, CHUNK, 1)
        )

    def turn(values):
        results = []
        for j in range(4):
            result = None
            for l in range(4):
                moved = values[l] if l == j else pltpu.roll(values[l], 32 * (l - j) % 128, 1)
                result = moved if result is None else jnp.where(lane // 32 == l, moved, result)
            results.append(result)
        return results

    half = groups // 2
    quarter = groups // 4
    pl.semaphore_wait(barrier, PEN + pair)
    loads[0].wait()
    place = (
        lax.broadcasted_iota(jnp.int32, (CHUNK, 128), 1) % CHUNK
        == lax.broadcasted_iota(jnp.int32, (CHUNK, 128), 0)
    ).astype(F32)
    placed = lax.dot_general(
        bs[...].reshape(6 * LEVELS * rows_y, CHUNK), place, (((1,), (0,)), ((), ())),
        precision=lax.Precision.HIGHEST, preferred_element_type=F32,
    ).reshape(6, LEVELS, rows_y, 128)
    for q in range(3):
        result = placed[2 * q, 0]
        for group in range(1, 8):
            result = jnp.where(
                lane // CHUNK == group, placed[2 * q + group % 2, group // 2], result
            )
        bb[pair, core, :, 128 * q : 128 * (q + 1)] = result

    def lanes(piece):
        return slice(256 * piece, 256 + 128 * piece)

    def gather(target, piece):
        arrival = pair // quarter if piece == 0 else 4 + pair // half
        return pltpu.make_async_remote_copy(
            src_ref=bb.at[pair, core, :, lanes(piece)],
            dst_ref=bb.at[pair, core, :, lanes(piece)],
            send_sem=hs.at[0],
            recv_sem=hr.at[arrival],
            device_id=(target * 2 + core, pen),
            device_id_type=MESH,
        )

    def pieces(count, piece, sem):
        return pltpu.make_async_remote_copy(
            src_ref=bb.at[:count, 0, :, lanes(piece)],
            dst_ref=bb.at[:count, 0, :, lanes(piece)],
            send_sem=hs.at[0],
            recv_sem=sem,
            device_id=(other, pen),
            device_id_type=MESH,
        )

    def swap(piece, part, size, side):
        block = bb.at[size * part : size * (part + 1), side, :, lanes(piece)]
        return pltpu.make_async_remote_copy(
            src_ref=block,
            dst_ref=block,
            send_sem=cs.at[0],
            recv_sem=cr.at[piece],
            device_id=(other, pen),
            device_id_type=MESH,
        )

    def collect(piece):
        size = quarter if piece == 0 else half
        for part in range(groups // size):
            arrival = hr.at[4 * piece + part]

            @pl.when(pair // size == part)
            def _():
                pieces(size - 1, piece, arrival).wait_recv()

            @pl.when(pair // size != part)
            def _():
                pieces(size, piece, arrival).wait_recv()

            swap(piece, part, size, core).start()

    for piece in range(2):
        for target in range(groups - 1):

            @pl.when(target < pair)
            def _():
                gather(target, piece).start()

    for k in range(1, groups):

        @pl.when(pair - k >= 0)
        def _():
            pl.semaphore_signal(
                here.at[pair // half],
                inc=1,
                device_id=((pair - k) * 2 + core, pen),
                device_id_type=MESH,
            )

    kappa_y, signed_y = wave_numbers((ROWS, 1), 0, pen * ROWS)
    kappa_x, signed_x = wave_numbers((1, GRID), 1, 0)
    wave_square = signed_y * signed_y + signed_x * signed_x
    factor = (2.0 * math.pi / GRID) ** 2
    square = factor * wave_square.astype(F32)
    inverse = jnp.where(
        wave_square > 0, 1.0 / (factor * jnp.maximum(wave_square, 1).astype(F32)), 0.0
    )

    loads[1].wait()
    loads[2].wait()

    packed = []
    for level in range(LEVELS):
        zr, zi = st[0, level, :, :GRID], st[0, level, :, GRID:]
        tr, ti = st[1, level, :, :GRID], st[1, level, :, GRID:]
        wzr, wzi = kappa_x * zr - kappa_y * zi, kappa_x * zi + kappa_y * zr
        wtr, wti = kappa_x * tr - kappa_y * ti, kappa_x * ti + kappa_y * tr
        packed += [wzr * inverse, -wzi, -wti, wzi * inverse, wzr, wtr]
    pk_high[...], pk_low[...] = split(jnp.concatenate(packed, axis=0))

    def forward(target, piece):
        at = slice(2 * piece, 2 + piece)
        return pltpu.make_async_remote_copy(
            src_ref=xs.at[target, at],
            dst_ref=g.at[pen, at],
            send_sem=fs.at[0],
            recv_sem=fr.at[piece],
            device_id=(ens, target),
            device_id_type=MESH,
        )

    for m in (2, 1, 3, 0):
        to = (column + m) % 4
        at = pl.ds(pl.multiple_of(to * 128, 128), 128)
        mixed = product((pk_high[...], pk_low[...]), (wide[0, :, at], wide[1, :, at]))
        mixed = mixed.reshape(LEVELS, 2, 3 * ROWS, 128)
        parts = turn([mixed[l, 0] + sign * swap_parts(mixed[l, 1]) for l in range(LEVELS)])
        for j in range(4):
            xs[to * 4 + j] = parts[j].reshape(3, ROWS, 128)
        for k in (2, 1, 3, 0):
            if k != 0 or m != 0:
                forward(to * 4 + (row + k) % 4, 0).start()
    for m in (2, 1, 3, 0):
        for k in (2, 1, 3, 0):
            if k != 0 or m != 0:
                forward((column + m) % 4 * 4 + (row + k) % 4, 1).start()
    g[pen] = xs[pen]
    for part in range(2):
        waits = jnp.where(pair // half == part, half * (part + 1) - 1 - pair, half)
        waits = jnp.where(pair // half > part, 0, waits)

        @pl.when(waits > 0)
        def _():
            pl.semaphore_wait(here.at[part], waits)

        for piece in range(2):
            for target in range(half * part, half * (part + 1)):

                @pl.when(pair < target)
                def _():
                    gather(target, piece).start()

    loads[4].wait()
    for level in range(LEVELS):
        up, down = min(level + 1, LEVELS - 1), max(level - 1, 0)
        zr, zi = st[0, level, :, :GRID], st[0, level, :, GRID:]
        tr, ti = st[1, level, :, :GRID], st[1, level, :, GRID:]
        across = stratification * kappa_x * inverse
        linear = (
            jnp.concatenate([-buoyancy_gain * kappa_x * ti, buoyancy_gain * kappa_x * tr], axis=1),
            jnp.concatenate([-across * zi, across * zr], axis=1),
        )
        damping = viscosity * jnp.concatenate([square, square], axis=1)
        for field in range(2):
            value = st[field, level]
            mixing = st[field, up] + st[field, down] - 2.0 * value
            lin[field, 0, level] = (
                memory_factor * ac[field, level]
                + linear[field]
                - damping * value
                + vertical_mixing * mixing
            )

    def others(sent, received, send_sem, recv_sem):
        return pltpu.make_async_remote_copy(
            src_ref=sent.at[: PEN - 1],
            dst_ref=received.at[: PEN - 1],
            send_sem=send_sem.at[0],
            recv_sem=recv_sem,
            device_id=(other, pen),
            device_id_type=MESH,
        )

    def blocks(value, part):
        rows = value.reshape(value.shape[0] // 32, 2, CHUNK, 128)[:, part]
        return rows.reshape(value.shape[0] // 2, 128)

    def turn_y(fields):
        spectral = jnp.concatenate([g[:, f].reshape(GRID, 128) for f in fields], axis=1)
        turned = product((tall[0], tall[1]), split(spectral))
        ones = [turned[:, 128 * i : 128 * (i + 1)] for i in range(len(fields))]
        return [blocks(one, 0) + sign * swap_parts(blocks(one, 1)) for one in ones]

    def base(q):
        return bb[:, :, :, 128 * q : 128 * (q + 1)].reshape(GRID, 128)

    def base_swapped(piece):
        whole = bb.at[:, 0, :, lanes(piece)]
        return pltpu.make_async_remote_copy(
            src_ref=whole,
            dst_ref=whole,
            send_sem=cs.at[0],
            recv_sem=cr.at[piece],
            device_id=(other, pen),
            device_id_type=MESH,
        )

    def backward(target, field):
        return pltpu.make_async_remote_copy(
            src_ref=ys.at[target, field],
            dst_ref=h.at[pen, field],
            send_sem=rs.at[0],
            recv_sem=rr.at[field],
            device_id=(ens, target),
            device_id_type=MESH,
        )

    def send_back(field, terms):
        adverse = split(terms + swap_parts(terms))
        for m in (2, 1, 3, 0):
            to = (column + m) % 4
            rows = pl.ds(pl.multiple_of(to * 128, 128), 128)
            spread_y = product((tall[0, rows], tall[1, rows]), adverse)
            result = jnp.where(first, blocks(spread_y, 0), -blocks(spread_y, 1))
            ys[pl.ds(to * 4, 4), field] = result.reshape(4, ROWS, 128)
            for k in (2, 1, 3, 0):
                if k != 0 or m != 0:
                    backward(to * 4 + (row + k) % 4, field).start()
        h[pen, field] = ys[pen, field]


    def finish(field):
        others(ys.at[:, field], h.at[:, field], rs, rr.at[field]).wait_recv()
        turned_x = [turn([h[4 * q + j, field] for j in range(4)]) for q in range(4)]
        rows = [
            jnp.concatenate([turned_x[q][level] for level in range(LEVELS)], axis=0)
            for q in range(4)
        ]
        gathered_x = jnp.concatenate(
            [jnp.concatenate(rows, axis=1),
             jnp.concatenate([-sign * swap_parts(one) for one in rows], axis=1)], axis=0
        )
        spectra = product(split(gathered_x), (tall[0], tall[1]))
        for level in range(LEVELS):
            for part in range(2):
                at = slice(GRID * part, GRID * (part + 1))
                start = (LEVELS * part + level) * ROWS
                advected[field, 0, level, :, at] = spectra[start : start + ROWS]

    collect(0)
    loads[3].wait()
    others(xs.at[:, 0:2], g.at[:, 0:2], fs, fr.at[0]).wait_recv()
    flow, vort_slopes = turn_y((0, 1))
    base_swapped(0).wait_recv()
    send_back(0, base(0) * vort_slopes + base(1) * flow)
    collect(1)
    others(xs.at[:, 2:3], g.at[:, 2:3], fs, fr.at[1]).wait_recv()
    (buoy_slopes,) = turn_y((2,))
    base_swapped(1).wait_recv()
    send_back(1, base(0) * buoy_slopes + base(2) * flow)
    finish(0)
    finish(1)

    for piece in range(2):
        pieces(groups - 1, piece, hr.at[0]).wait_send()
        base_swapped(piece).wait_send()
    others(xs, g, fs, fr.at[0]).wait_send()
    others(ys, h, rs, rr.at[0]).wait_send()


def on_device(groups, state, accum, base_flow):
    rows_y = GRID // (2 * groups)
    wide, tall = tables()
    fields = (2, LEVELS, ROWS, 2 * GRID)
    result = jax.ShapeDtypeStruct(state.shape, F32)
    dma = pltpu.SemaphoreType.DMA
    linear, advected = pl.pallas_call(
        functools.partial(kernel, groups),
        out_shape=(result, result),
        in_specs=[pl.BlockSpec(memory_space=pltpu.HBM)] * 5,
        out_specs=(pl.BlockSpec(memory_space=pltpu.VMEM),) * 2,
        scratch_shapes=[
            pltpu.VMEM(fields, F32),
            pltpu.VMEM(fields, F32),
            pltpu.VMEM((6, LEVELS, rows_y, 16), F32),
            pltpu.VMEM((2, GRID, 2 * GRID), BF16),
            pltpu.VMEM((2, 2 * GRID, GRID), BF16),
            pltpu.VMEM((6 * LEVELS * ROWS, GRID), BF16),
            pltpu.VMEM((6 * LEVELS * ROWS, GRID), BF16),
            pltpu.VMEM((PEN, 3, ROWS, 128), F32),
            pltpu.VMEM((PEN, 3, ROWS, 128), F32),
            pltpu.VMEM((groups, 2, rows_y, 384), F32),
            pltpu.VMEM((PEN, 2, ROWS, 128), F32),
            pltpu.VMEM((PEN, 2, ROWS, 128), F32),
            dma((5,)),
            dma((1,)),
            dma((2,)),
            dma((1,)),
            dma((2,)),
            dma((1,)),
            dma((2,)),
            dma((1,)),
            dma((6,)),
            pltpu.SemaphoreType.REGULAR((2,)),
        ],
        compiler_params=pltpu.CompilerParams(
            collective_id=0, has_side_effects=True, vmem_limit_bytes=40 * 1024 * 1024
        ),
        name="step",
    )(*[pltpu.with_memory_space_constraint(x, pltpu.HBM) for x in (
        state.reshape(fields), accum.reshape(fields), base_flow.transpose(0, 1, 3, 2),
        jnp.asarray(wide), jnp.asarray(tall))]
    )
    accum_next = linear - advected
    return state + weight_factor * time_step * accum_next, accum_next


def solution(mesh):
    spectral = P(None, "ens", None, "pen", None)
    return jax.shard_map(
        functools.partial(on_device, mesh.shape["ens"] // 2),
        mesh=mesh,
        in_specs=(spectral, spectral, P(None, None, "pen", "ens")),
        out_specs=(spectral, spectral),
        check_vma=False,
    )
```

time: 35.4 us -> 34.6 us (0.977)
  local copies, waits for them, and re-layouts: 1.41 us -> 0.01 us
  other arithmetic: 0 us -> 0.86 us
    unnamed x2, local copies, waits for them, and re-layouts: 1.41 us -> 0.01 us
    add x0 -> x1, other arithmetic: none -> 0.86 us  [on_device(): return (state + weight_factor * time_step * accum_next, accum_next)]
where the time goes in v5:
time: 34.6 us; the launch traced here: 34.5 us
  Pallas kernels  33 us (95%)
  other arithmetic  0.86 us (2%)
  between operations  0.65 us (2%)
    pallas_call x1, Pallas kernels, on_device(): pl.pallas_call(functools.partial(kernel, groups), out_shape=(result, resu...  33 us
    add x1, other arithmetic, on_device(): return (state + weight_factor * time_step * accum_next, accum_next)  0.86 us

profile of v5, /device:TPU:1, one launch (start us, length us, event | category | flops | bytes accessed | tf_op | source)
XLA Modules:
  0.0 34.5 jit_solution(18336454761253891911)
XLA Ops:
  0.6 0.0 copy-start
  0.6 33.0 %step.1 = (f32[2,1,4,16,512]{4,3,2,1,0:T(8,128)S(1)}, f32[2,1,4,16,512]{4,3,2,1,0:T(8,128)S(1)}) custom-call(f32[2,4,16,512]{3,2,1,0:T(8,128)} %bitcast.3, f32[2,4,16,512]{3,2,1,0:T(8,128)} %bitcast.4, f32[6,4,8,16]{3,2,1,0:T(8,128)} %bitcast.5, bf16[2,256,512]{2,1,0:T(8,128)(2,1)} %constant.6.clone.wide_hbm, bf16[2,512,256]{2,1,0:T(8,128)(2,1)} %constant.7.clone.tall_hbm), custom_call_target="tpu_custom_call" | custom-call | tf_op jit(solution)/shard_map/step/pallas_call | solution.py:393
  33.6 0.0 copy-done
  33.6 0.9 %multiply_add_fusion = (f32[2,1,4,16,512]{4,3,2,1,0:T(8,128)}, f32[2,1,4,16,512]{4,3,2,1,0:T(8,128)}) fusion(f32[2,1,4,16,512]{4,3,2,1,0:T(8,128)S(1)} %copy-done, f32[2,1,4,16,512]{4,3,2,1,0:T(8,128)S(1)} %get-tuple-element.4, f32[2,1,4,16,512]{4,3,2,1,0:T(8,128)S(1)} %get-tuple-element.5), kind=kLoop, calls=%fused_computation | loop fusion | flops 196608 | bytes 1310720 | tf_op jit(solution)/shard_map/add | solution.py:431
Async XLA Ops:
  0.6 33.0 %copy-start = (f32[2,1,4,16,512]{4,3,2,1,0:T(8,128)S(1)}, f32[2,1,4,16,512]{4,3,2,1,0:T(8,128)}, u32[]{:S(2)}) copy-start(f32[2,1,4,16,512]{4,3,2,1,0:T(8,128)} %param.5) | copy-start | bytes 786436

commit v6 on v5

--- a/solution.py
+++ b/solution.py
@@ -118,6 +118,17 @@
     half = groups // 2
     quarter = groups // 4
     pl.semaphore_wait(barrier, PEN + pair)
+    for k in range(1, groups):
+
+        @pl.when(pair - k >= 0)
+        def _():
+            pl.semaphore_signal(
+                here.at[pair // half],
+                inc=1,
+                device_id=((pair - k) * 2 + core, pen),
+                device_id_type=MESH,
+            )
+
     loads[0].wait()
     place = (
         lax.broadcasted_iota(jnp.int32, (CHUNK, 128), 1) % CHUNK
@@ -191,17 +202,6 @@
             @pl.when(target < pair)
             def _():
                 gather(target, piece).start()
-
-    for k in range(1, groups):
-
-        @pl.when(pair - k >= 0)
-        def _():
-            pl.semaphore_signal(
-                here.at[pair // half],
-                inc=1,
-                device_id=((pair - k) * 2 + core, pen),
-                device_id_type=MESH,
-            )
 
     kappa_y, signed_y = wave_numbers((ROWS, 1), 0, pen * ROWS)
     kappa_x, signed_x = wave_numbers((1, GRID), 1, 0)

time: 34.6 us -> 34.5 us (level)
  no operation moved by 1% of the time
where the time goes in v6:
time: 34.5 us; the launch traced here: 34.3 us
  Pallas kernels  32.8 us (95%)
  other arithmetic  0.86 us (2%)
  between operations  0.65 us (2%)
    pallas_call x1, Pallas kernels, on_device(): pl.pallas_call(functools.partial(kernel, groups), out_shape=(result, resu...  32.8 us
    add x1, other arithmetic, on_device(): return (state + weight_factor * time_step * accum_next, accum_next)  0.86 us

profile of v6, /device:TPU:1, one launch (start us, length us, event | category | flops | bytes accessed | tf_op | source)
XLA Modules:
  0.0 34.3 jit_solution(12701052160304777320)
XLA Ops:
  0.6 0.0 copy-start
  0.6 32.8 %step.1 = (f32[2,1,4,16,512]{4,3,2,1,0:T(8,128)S(1)}, f32[2,1,4,16,512]{4,3,2,1,0:T(8,128)S(1)}) custom-call(f32[2,4,16,512]{3,2,1,0:T(8,128)} %bitcast.3, f32[2,4,16,512]{3,2,1,0:T(8,128)} %bitcast.4, f32[6,4,8,16]{3,2,1,0:T(8,128)} %bitcast.5, bf16[2,256,512]{2,1,0:T(8,128)(2,1)} %constant.6.clone.wide_hbm, bf16[2,512,256]{2,1,0:T(8,128)(2,1)} %constant.7.clone.tall_hbm), custom_call_target="tpu_custom_call" | custom-call | tf_op jit(solution)/shard_map/step/pallas_call | solution.py:393
  33.5 0.0 copy-done
  33.5 0.9 %multiply_add_fusion = (f32[2,1,4,16,512]{4,3,2,1,0:T(8,128)}, f32[2,1,4,16,512]{4,3,2,1,0:T(8,128)}) fusion(f32[2,1,4,16,512]{4,3,2,1,0:T(8,128)S(1)} %copy-done, f32[2,1,4,16,512]{4,3,2,1,0:T(8,128)S(1)} %get-tuple-element.4, f32[2,1,4,16,512]{4,3,2,1,0:T(8,128)S(1)} %get-tuple-element.5), kind=kLoop, calls=%fused_computation | loop fusion | flops 196608 | bytes 1310720 | tf_op jit(solution)/shard_map/add | solution.py:431
Async XLA Ops:
  0.6 32.8 %copy-start = (f32[2,1,4,16,512]{4,3,2,1,0:T(8,128)S(1)}, f32[2,1,4,16,512]{4,3,2,1,0:T(8,128)}, u32[]{:S(2)}) copy-start(f32[2,1,4,16,512]{4,3,2,1,0:T(8,128)} %param.5) | copy-start | bytes 786436

commit v7 on v6

--- a/solution.py
+++ b/solution.py
@@ -88,13 +88,11 @@
     for k in range(1, PEN):
         pl.semaphore_signal(barrier, inc=1, device_id=(ens, (pen + k) % PEN), device_id_type=MESH)
     pl.semaphore_signal(barrier, inc=1, device_id=(other, pen), device_id_type=MESH)
-    for k in range(1, groups):
-
-        @pl.when(pair + k < groups)
-        def _():
-            pl.semaphore_signal(
-                barrier, inc=1, device_id=((pair + k) * 2 + core, pen), device_id_type=MESH
-            )
+    @pl.loop(pair + 1, groups)
+    def _(target):
+        pl.semaphore_signal(
+            barrier, inc=1, device_id=(target * 2 + core, pen), device_id_type=MESH
+        )
 
     lane = lax.broadcasted_iota(jnp.int32, (1, 128), 1)
     first = lane // CHUNK % 2 == 0
@@ -118,16 +116,11 @@
     half = groups // 2
     quarter = groups // 4
     pl.semaphore_wait(barrier, PEN + pair)
-    for k in range(1, groups):
-
-        @pl.when(pair - k >= 0)
-        def _():
-            pl.semaphore_signal(
-                here.at[pair // half],
-                inc=1,
-                device_id=((pair - k) * 2 + core, pen),
-                device_id_type=MESH,
-            )
+    @pl.loop(0, pair)
+    def _(target):
+        pl.semaphore_signal(
+            here.at[pair // half], inc=1, device_id=(target * 2 + core, pen), device_id_type=MESH
+        )
 
     loads[0].wait()
     place = (
@@ -197,11 +190,9 @@
             swap(piece, part, size, core).start()
 
     for piece in range(2):
-        for target in range(groups - 1):
-
-            @pl.when(target < pair)
-            def _():
-                gather(target, piece).start()
+        @pl.loop(0, pair)
+        def _(target):
+            gather(target, piece).start()
 
     kappa_y, signed_y = wave_numbers((ROWS, 1), 0, pen * ROWS)
     kappa_x, signed_x = wave_numbers((1, GRID), 1, 0)

time: 34.5 us -> 34.6 us (level)
  no operation moved by 1% of the time
where the time goes in v7:
time: 34.6 us; the launch traced here: 34.5 us
  Pallas kernels  33 us (95%)
  other arithmetic  0.86 us (2%)
  between operations  0.65 us (2%)
    pallas_call x1, Pallas kernels, on_device(): pl.pallas_call(functools.partial(kernel, groups), out_shape=(result, resu...  33 us
    add x1, other arithmetic, on_device(): return (state + weight_factor * time_step * accum_next, accum_next)  0.86 us

profile of v7, /device:TPU:1, one launch (start us, length us, event | category | flops | bytes accessed | tf_op | source)
XLA Modules:
  0.0 34.5 jit_solution(10035406191467327221)
XLA Ops:
  0.6 0.0 copy-start
  0.6 33.0 %step.1 = (f32[2,1,4,16,512]{4,3,2,1,0:T(8,128)S(1)}, f32[2,1,4,16,512]{4,3,2,1,0:T(8,128)S(1)}) custom-call(f32[2,4,16,512]{3,2,1,0:T(8,128)} %bitcast.3, f32[2,4,16,512]{3,2,1,0:T(8,128)} %bitcast.4, f32[6,4,8,16]{3,2,1,0:T(8,128)} %bitcast.5, bf16[2,256,512]{2,1,0:T(8,128)(2,1)} %constant.6.clone.wide_hbm, bf16[2,512,256]{2,1,0:T(8,128)(2,1)} %constant.7.clone.tall_hbm), custom_call_target="tpu_custom_call" | custom-call | tf_op jit(solution)/shard_map/step/pallas_call | solution.py:384
  33.6 0.0 copy-done
  33.6 0.9 %multiply_add_fusion = (f32[2,1,4,16,512]{4,3,2,1,0:T(8,128)}, f32[2,1,4,16,512]{4,3,2,1,0:T(8,128)}) fusion(f32[2,1,4,16,512]{4,3,2,1,0:T(8,128)S(1)} %copy-done, f32[2,1,4,16,512]{4,3,2,1,0:T(8,128)S(1)} %get-tuple-element.4, f32[2,1,4,16,512]{4,3,2,1,0:T(8,128)S(1)} %get-tuple-element.5), kind=kLoop, calls=%fused_computation | loop fusion | flops 196608 | bytes 1310720 | tf_op jit(solution)/shard_map/add | solution.py:422
Async XLA Ops:
  0.6 33.0 %copy-start = (f32[2,1,4,16,512]{4,3,2,1,0:T(8,128)S(1)}, f32[2,1,4,16,512]{4,3,2,1,0:T(8,128)}, u32[]{:S(2)}) copy-start(f32[2,1,4,16,512]{4,3,2,1,0:T(8,128)} %param.5) | copy-start | bytes 786436
